TPU v7x, 32 devices: a whole 2x2x4 slice. The times are simulated.
32 devices in a mesh: pln: 8 (over y, x, core), pen: 4 (over z).
Axes of the slice: x: 2, y: 2, z: 4, core: 2. Of those that a mesh axis runs over, the one named last changes fastest.
Arguments:
- block_owner: int32 [4096, 1], P(('pln', 'pen')), may hold values from 0 to 31; in each aligned block of 128 rows (0 to 127, 128 to 255, ...) at most 8 rows name the same one
- block_band: int32 [4096], P(('pln', 'pen')), may hold values from 0 to 31
- block_count: int32 [4096], P(('pln', 'pen')), may hold values from 1 to 128
- cells: int32 [4096, 128], P(('pln', 'pen')), may hold values from 0 to 8191
- offsets: float32 [4096, 2, 128], P(('pln', 'pen')), may hold values from 0 to 1
- charges: float32 [4096, 128], P(('pln', 'pen')), may hold values from -5 to 5
Outputs:
- potential: float32 [8, 1024, 1024], P('pln', 'pen')
- forces: float32 [4096, 2, 128], P(('pln', 'pen'))
Inputs may be any that keep to these rules, and one draw needn't show every extreme that they name: `block_owner`: among the blocks of one device no owner is named more than 8 times, a bound that some block reaches.
All inputs are finite; a program needn't handle non-finite values.
Results may differ from a plain program's by a relative error of at most 0.0044.
Values sent between devices are 32-bit elements; how exact they have to be, the bound alone decides.
A program may use at most 64 MiB of HBM per device.

v0:
```python
import functools
import math

import jax
import jax.numpy as jnp
import numpy as np
from jax import lax
from jax.experimental import pallas as pl
from jax.experimental.pallas import tpu as pltpu
from jax.sharding import PartitionSpec as P

NG = 1024
LANES = 128
CHUNKS = NG // LANES
screening = 2e-05
VMEM_LIMIT = 48 * 1024 * 1024
UNROLL = 4


def round_up(value, step):
    return -(-value // step) * step


@functools.lru_cache(None)
def hartley_tables():
    index = np.arange(NG)
    angle = 2.0 * np.pi / NG * (index[:, None] * index[None, :] % NG)
    table = np.cos(angle) + np.sin(angle)
    high = table.astype(jnp.bfloat16)
    low = (table - high.astype(np.float64)).astype(jnp.bfloat16)
    return high, low


@functools.lru_cache(None)
def line_tables(pen_count):
    rows = NG // pen_count
    shift = 4.0 * np.sin(np.pi * np.arange(NG) / NG) ** 2 + screening
    root = 1.0 + shift / 2.0 - np.sqrt(shift + shift * shift / 4.0)
    i = np.arange(8)[:, None]

    def power(exponent):
        return root[None, :] ** (exponent + np.zeros((8, 1)))

    tiles = [
        power(7 - i),
        power(i),
        power(8),
        np.where(i >= 1, power(1), 0.0),
        np.where(i >= 2, power(2), 0.0),
        np.where(i >= 4, power(4), 0.0),
        np.where(i <= 6, power(1), 0.0),
        np.where(i <= 5, power(2), 0.0),
        np.where(i <= 3, power(4), 0.0),
        power(i + 1),
        power(8 - i),
        np.broadcast_to(1.0 / ((1.0 / root - root) * NG), (8, NG)),
        np.broadcast_to(2.0 + shift, (8, NG)),
        power(rows - 1),
    ]
    lags = np.arange(round_up(pen_count, 8))[:, None]
    tiles.append(root[None, :] ** (lags * rows) / (1.0 - root[None, :] ** NG))
    return np.concatenate(tiles, axis=0).astype(np.float32)


T_FEND, T_BEND, T_EIGHT, T_F1, T_F2, T_F4, T_B1, T_B2, T_B4, T_FC, T_BC, T_NORM, T_DIAG, T_LAST, T_LAG = range(15)


def fetch(sources, targets, sems):
    copies = [pltpu.make_async_copy(a, b, sems.at[i]) for i, (a, b) in enumerate(zip(sources, targets))]
    for copy in copies:
        copy.start()
    return copies


def pack_kernel(capacity, owner_h, band_h, count_h, cells_h, offsets_h, charges_h, out, target,
                owner, band, count, cells, offsets, charges, used, sems):
    devices = out.shape[0]
    copies = fetch(
        (owner_h, band_h, count_h, cells_h, offsets_h, charges_h),
        (owner, band, count, cells, offsets, charges),
        sems,
    )
    empty = 4 * capacity
    out[...] = jnp.full(out.shape, -1.0, jnp.float32)
    out[:, 0:empty, :] = jnp.zeros((devices, empty, LANES), jnp.float32)

    def clear(i, carry):
        used[i] = 0
        return carry

    lax.fori_loop(0, devices, clear, 0)
    lane = lax.broadcasted_iota(jnp.int32, (1, LANES), 1)
    for copy in copies:
        copy.wait()

    def place(i, carry):
        o = owner[i]
        j = used[o]
        used[o] = j + 1
        target[i] = o * capacity + j
        pair = offsets[i]
        out[o, pl.ds(j, 1), :] = pair[0:1]
        out[o, pl.ds(capacity + j, 1), :] = pair[1:2]
        out[o, pl.ds(2 * capacity + j, 1), :] = jnp.where(lane < count[i], charges[pl.ds(i, 1), :], 0.0)
        out[o, pl.ds(3 * capacity + j, 1), :] = cells[pl.ds(i, 1), :].astype(jnp.float32)
        out[o, pl.ds(4 * capacity + j, 1), :] = jnp.full((1, LANES), band[i], jnp.int32).astype(jnp.float32)
        return carry

    lax.fori_loop(0, owner.shape[0], place, 0)


def peer(index, pens):
    return (lax.div(index, pens), lax.rem(index, pens))


def exchange_kernel(planes, pens, source, target, send_sems, recv_sems, own_sem):
    count = planes * pens
    me = lax.axis_index("pln") * pens + lax.axis_index("pen")
    barrier = pltpu.get_barrier_semaphore()

    def greet(k, carry):
        other = peer(lax.rem(me + k, count), pens)
        pl.semaphore_signal(barrier, inc=1, device_id=other, device_id_type=pl.DeviceIdType.MESH)
        return carry

    own = pltpu.make_async_copy(source.at[me], target.at[me], own_sem)
    own.start()
    lax.fori_loop(1, count, greet, 0)
    pl.semaphore_wait(barrier, count - 1)

    def copy_to(k):
        to = lax.rem(me + k, count)
        return pltpu.make_async_remote_copy(
            src_ref=source.at[to],
            dst_ref=target.at[me],
            send_sem=send_sems.at[k],
            recv_sem=recv_sems.at[k],
            device_id=peer(to, pens),
            device_id_type=pl.DeviceIdType.MESH,
        )

    def send(k, carry):
        copy_to(k).start()
        return carry

    def finish(k, carry):
        copy_to(k).wait_send()
        pltpu.make_async_remote_copy(
            src_ref=source.at[me],
            dst_ref=target.at[lax.rem(me - k + count, count)],
            send_sem=send_sems.at[k],
            recv_sem=recv_sems.at[k],
            device_id=peer(lax.rem(me - k + count, count), pens),
            device_id_type=pl.DeviceIdType.MESH,
        ).wait_recv()
        return carry

    lax.fori_loop(1, count, send, 0)
    lax.fori_loop(1, count, finish, 0)
    own.wait()


def exchange(values, planes, pens, number):
    place = pl.BlockSpec(memory_space=pl.ANY)
    return pl.pallas_call(
        functools.partial(exchange_kernel, planes, pens),
        out_shape=jax.ShapeDtypeStruct(values.shape, values.dtype),
        in_specs=[place],
        out_specs=place,
        scratch_shapes=[
            pltpu.SemaphoreType.DMA((planes * pens,)),
            pltpu.SemaphoreType.DMA((planes * pens,)),
            pltpu.SemaphoreType.DMA,
        ],
        compiler_params=pltpu.CompilerParams(collective_id=number, has_side_effects=True),
        name="exchange",
    )(values)


def share_kernel(pens, source, target, send_sems, recv_sems, own_sem):
    mine = lax.axis_index("pen")
    plane = lax.axis_index("pln")
    barrier = pltpu.get_barrier_semaphore()
    own = pltpu.make_async_copy(source, target.at[mine], own_sem)
    own.start()
    for k in range(1, pens):
        other = (plane, lax.rem(mine + k, pens))
        pl.semaphore_signal(barrier, inc=1, device_id=other, device_id_type=pl.DeviceIdType.MESH)
    pl.semaphore_wait(barrier, pens - 1)
    sends = []
    for k in range(1, pens):
        copy = pltpu.make_async_remote_copy(
            src_ref=source,
            dst_ref=target.at[mine],
            send_sem=send_sems.at[k],
            recv_sem=recv_sems.at[k],
            device_id=(plane, lax.rem(mine + k, pens)),
            device_id_type=pl.DeviceIdType.MESH,
        )
        copy.start()
        sends.append(copy)
    for k in range(1, pens):
        sends[k - 1].wait_send()
        behind = lax.rem(mine - k + pens, pens)
        pltpu.make_async_remote_copy(
            src_ref=source,
            dst_ref=target.at[behind],
            send_sem=send_sems.at[k],
            recv_sem=recv_sems.at[k],
            device_id=(plane, behind),
            device_id_type=pl.DeviceIdType.MESH,
        ).wait_recv()
    own.wait()


def share(values, pens, number):
    place = pl.BlockSpec(memory_space=pltpu.VMEM)
    return pl.pallas_call(
        functools.partial(share_kernel, pens),
        out_shape=jax.ShapeDtypeStruct((pens,) + values.shape, values.dtype),
        in_specs=[place],
        out_specs=place,
        scratch_shapes=[
            pltpu.SemaphoreType.DMA((pens,)),
            pltpu.SemaphoreType.DMA((pens,)),
            pltpu.SemaphoreType.DMA,
        ],
        compiler_params=pltpu.CompilerParams(collective_id=number, has_side_effects=True),
        name="share",
    )(values)


def live_list(bands, live, capacity):
    total = bands.shape[0]

    def check(s, n):
        live[n] = s
        return n + jnp.where(bands[s] >= 0, 1, 0)

    return lax.fori_loop(0, total, check, jnp.int32(0))


def particle(recv, capacity, s):
    d = s // capacity
    j = s % capacity
    frac_x = recv[d, pl.ds(j, 1), :]
    frac_y = recv[d, pl.ds(capacity + j, 1), :]
    weight = recv[d, pl.ds(2 * capacity + j, 1), :]
    cell = recv[d, pl.ds(3 * capacity + j, 1), :].astype(jnp.int32)
    column = cell % NG
    after = (column + 1) % NG
    row = cell // NG
    left = (1.0 - frac_x).astype(jnp.bfloat16).astype(jnp.float32)
    right = frac_x.astype(jnp.bfloat16).astype(jnp.float32)
    return frac_y, weight, row, column, after, left, right


def dot3(a_high, a_low, b_high, b_low):
    dot = functools.partial(jnp.dot, preferred_element_type=jnp.float32)
    return dot(a_high, b_high) + (dot(a_high, b_low) + dot(a_low, b_high))


def split(values):
    high = values.astype(jnp.bfloat16)
    return high, (values - high.astype(jnp.float32)).astype(jnp.bfloat16)


def deposit_kernel(capacity, rows, bands, recv, table_high_h, table_low_h, lines_h, spectrum, edges,
                   live, dens, hi, lo, table_high, table_low, lines, sems):
    total = bands.shape[0]
    copies = fetch((table_high_h, table_low_h, lines_h), (table_high, table_low, lines), sems)
    n_live = live_list(bands, live, capacity)
    dens[...] = jnp.zeros(dens.shape, jnp.float32)
    sub8 = lax.broadcasted_iota(jnp.int32, (8, LANES), 0)
    sub_all = lax.broadcasted_iota(jnp.int32, (LANES, LANES), 0)

    def one(slot_at):
        alive = slot_at < n_live
        s = live[jnp.where(alive, slot_at, 0)]
        frac_y, weight, row, column, after, left, right = particle(recv, capacity, s)
        weight = jnp.where(alive, weight, 0.0)
        lower = (weight * (1.0 - frac_y)).astype(jnp.bfloat16).astype(jnp.float32)
        upper = (weight * frac_y).astype(jnp.bfloat16).astype(jnp.float32)
        main = jnp.where(row == sub8, lower, jnp.where(row + 1 == sub8, upper, 0.0))
        tail = jnp.where((sub8 == 0) & (row == 7), upper, 0.0)
        tall = jnp.concatenate([main, tail], axis=0)
        chunk = column // LANES
        chunk_after = after // LANES
        row_left = jnp.concatenate([jnp.where(chunk == a, tall, 0.0) for a in range(CHUNKS)], axis=0)
        row_right = jnp.concatenate([jnp.where(chunk_after == a, tall, 0.0) for a in range(CHUNKS)], axis=0)
        col_left = jnp.where(column % LANES == sub_all, left, 0.0)
        col_right = jnp.where(after % LANES == sub_all, right, 0.0)
        lhs = jnp.concatenate([row_left.astype(jnp.bfloat16), row_right.astype(jnp.bfloat16)], axis=1)
        rhs = jnp.concatenate([col_left.astype(jnp.bfloat16), col_right.astype(jnp.bfloat16)], axis=1)
        values = lax.dot_general(lhs, rhs, (((1,), (1,)), ((), ())), preferred_element_type=jnp.float32)
        return jnp.maximum(bands[s], 0), values

    def group(g, carry):
        results = [one(g * UNROLL + k) for k in range(UNROLL)]
        for band, values in results:
            start = pl.multiple_of(band * 8, 8)
            for a in range(CHUNKS):
                lanes = slice(a * LANES, (a + 1) * LANES)
                dens[pl.ds(start, 16), lanes] += values[a * 16 : (a + 1) * 16]
        return carry

    lax.fori_loop(0, (n_live + UNROLL - 1) // UNROLL, group, 0)
    high, low = split(dens[...])
    hi[...] = high
    lo[...] = low
    width = 256
    for copy in copies:
        copy.wait()
    for n in range(NG // width):
        cols = slice(n * width, (n + 1) * width)
        values = dot3(hi[...], lo[...], table_high[:, cols], table_low[:, cols])
        spectrum[:, cols] = values[:rows]
        edges[2:3, cols] = values[rows : rows + 1]
    eight = lines[T_EIGHT * 8 : T_EIGHT * 8 + 8]
    tiles = rows // 8

    def fold(t, carry):
        fwd, bwd = carry
        fwd = eight * fwd + spectrum[pl.ds(pl.multiple_of(t * 8, 8), 8), :]
        bwd = eight * bwd + spectrum[pl.ds(pl.multiple_of((tiles - 1 - t) * 8, 8), 8), :]
        return fwd, bwd

    nothing = jnp.zeros((8, NG), jnp.float32)
    fwd, bwd = lax.fori_loop(0, tiles, fold, (nothing, nothing))
    edges[0:1] = jnp.sum(fwd * lines[T_FEND * 8 : T_FEND * 8 + 8], axis=0, keepdims=True)
    edges[1:2] = jnp.sum(bwd * lines[T_BEND * 8 : T_BEND * 8 + 8], axis=0, keepdims=True)
    edges[3:5] = spectrum[0:2]
    edges[5:6] = spectrum[rows - 1 : rows]
    edges[6:8] = jnp.zeros((2, NG), jnp.float32)


def solve_kernel(capacity, rows, bands, place, recv, spectrum, gathered, table_high_h, table_low_h, lines_h, potential, forces,
                 live, wave, hi, lo, field, table_high, table_low, lines, sems):
    copies = fetch((lines_h, table_high_h, table_low_h), (lines, table_high, table_low), sems)
    copies[0].wait()
    pens = gathered.shape[0]
    mine = place[0]

    def table(which):
        return lines[which * 8 : which * 8 + 8]

    def row_of(pen, which):
        return gathered[lax.rem(pen + 2 * pens, pens), which : which + 1]

    last_power = table(T_LAST)[0:1]
    before = jnp.zeros((1, NG), jnp.float32)
    beyond = jnp.zeros((1, NG), jnp.float32)
    for j in range(pens):
        lag = lines[T_LAG * 8 + j : T_LAG * 8 + j + 1]
        behind, ahead = mine - 1 - j, mine + 1 + j
        before += lag * (row_of(behind, 0) + last_power * row_of(behind - 1, 2))
        beyond += lag * (row_of(ahead, 1) + row_of(ahead - 1, 2))
    incoming = row_of(mine - 1, 2)
    next_zero = row_of(mine + 1, 3) + row_of(mine, 2)
    next_one = row_of(mine + 1, 4)
    last_before = row_of(mine - 1, 5)
    spectrum_first = spectrum[0:1] + incoming
    first_row = lax.broadcasted_iota(jnp.int32, (8, NG), 0) == 0
    tiles = rows // 8

    def tile_of(t):
        values = spectrum[pl.ds(pl.multiple_of(t * 8, 8), 8), :]
        return values + jnp.where(first_row & (t == 0), incoming, 0.0)

    def backward(i, carry):
        t = tiles - 1 - i
        x = tile_of(t)
        x = x + table(T_B1) * pltpu.roll(x, 7, 0)
        x = x + table(T_B2) * pltpu.roll(x, 6, 0)
        x = x + table(T_B4) * pltpu.roll(x, 4, 0)
        x = x + table(T_BC) * carry
        wave[pl.ds(pl.multiple_of(t * 8 + 8, 8), 8), :] = x
        return x[0:1]

    first_back = lax.fori_loop(0, tiles, backward, beyond)
    norm = table(T_NORM)[0:1]

    def forward(t, carry):
        d = tile_of(t)
        x = d + table(T_F1) * pltpu.roll(d, 1, 0)
        x = x + table(T_F2) * pltpu.roll(x, 2, 0)
        x = x + table(T_F4) * pltpu.roll(x, 4, 0)
        x = x + table(T_FC) * carry
        where = pl.ds(pl.multiple_of(t * 8 + 8, 8), 8)
        wave[where, :] = table(T_NORM) * (x + wave[where, :] - d)
        return x[7:8]

    final = lax.fori_loop(0, tiles, forward, before)
    diagonal = table(T_DIAG)[0:1]
    root = table(T_FC)[0:1]
    scale = 1.0 / NG
    up1 = norm * (before + root * first_back)
    up2 = diagonal * up1 - wave[8:9] - scale * last_before
    down0 = norm * (root * final + beyond)
    down1 = diagonal * down0 - wave[rows + 7 : rows + 8] - scale * next_zero
    down2 = diagonal * down1 - down0 - scale * next_one
    wave[0:6] = jnp.zeros((6, NG), jnp.float32)
    wave[6:7] = up2
    wave[7:8] = up1
    wave[rows + 8 : rows + 9] = down0
    wave[rows + 9 : rows + 10] = down1
    wave[rows + 10 : rows + 11] = down2
    wave[rows + 11 : rows + 16] = jnp.zeros((5, NG), jnp.float32)
    high, low = split(wave[...])
    hi[...] = high
    lo[...] = low
    width = 256
    copies[1].wait()
    copies[2].wait()
    for n in range(NG // width):
        cols = slice(n * width, (n + 1) * width)
        wave[:, cols] = dot3(hi[...], lo[...], table_high[:, cols], table_low[:, cols])
    potential[...] = wave[8 : rows + 8]

    def derive(t, carry):
        base = pl.multiple_of(t * 8, 8)
        tall = jnp.concatenate(
            [
                wave[pl.ds(base, 8), :],
                wave[pl.ds(pl.multiple_of(base + 8, 8), 8), :],
                wave[pl.ds(pl.multiple_of(jnp.minimum(base + 16, rows + 8), 8), 8), :],
            ],
            axis=0,
        )
        middle = tall[8:16]
        along_x = (8.0 * (pltpu.roll(middle, NG - 1, 1) - pltpu.roll(middle, 1, 1))
                   - (pltpu.roll(middle, NG - 2, 1) - pltpu.roll(middle, 2, 1))) / -12.0
        along_y = (8.0 * (tall[9:17] - tall[7:15]) - (tall[10:18] - tall[6:14])) / -12.0

        @pl.when(t < tiles)
        def _():
            field[t, 0:8, :] = along_x
            field[t, 8:16, :] = along_y

        @pl.when(t > 0)
        def _():
            field[t - 1, 16:17, :] = along_x[0:1]
            field[t - 1, 17:18, :] = along_y[0:1]

        return carry

    lax.fori_loop(0, tiles + 1, derive, 0)
    for t in range(tiles):
        field[t, 18:24, :] = jnp.zeros((6, NG), jnp.float32)

    n_live = live_list(bands, live, capacity)
    forces[...] = jnp.zeros(forces.shape, jnp.float32)
    sub8 = lax.broadcasted_iota(jnp.int32, (8, LANES), 0)

    def pick(values, index):
        return jnp.take_along_axis(values, index, axis=1, mode="promise_in_bounds")

    def one(slot_at):
        s = live[jnp.minimum(slot_at, n_live - 1)]
        band = bands[s]
        frac_y, weight, row, column, after, left, right = particle(recv, capacity, s)
        index = jnp.broadcast_to(column % LANES, (8, LANES))
        index_after = jnp.broadcast_to(after % LANES, (8, LANES))
        chunk = jnp.broadcast_to(column // LANES, (8, LANES))
        chunk_after = jnp.broadcast_to(after // LANES, (8, LANES))
        mixed = []
        for part in range(3):
            near = jnp.zeros((8, LANES), jnp.float32)
            far = near
            for a in range(CHUNKS):
                values = field[band, part * 8 : part * 8 + 8, a * LANES : (a + 1) * LANES]
                near = jnp.where(chunk == a, pick(values, index), near)
                far = jnp.where(chunk_after == a, pick(values, index_after), far)
            mixed.append(left * near + right * far)
        row_weight = jnp.where(row == sub8, 1.0 - frac_y, jnp.where(row + 1 == sub8, frac_y, 0.0))
        edge = jnp.where(row == 7, frac_y, 0.0)
        out = [
            weight * (jnp.sum(row_weight * mixed[c], axis=0, keepdims=True) + edge * mixed[2][c : c + 1])
            for c in range(2)
        ]
        return s, out

    def group(g, carry):
        results = [one(g * UNROLL + k) for k in range(UNROLL)]
        for s, values in results:
            d = s // capacity
            j = s % capacity
            forces[d, pl.ds(j, 1), :] = values[0]
            forces[d, pl.ds(capacity + j, 1), :] = values[1]
        return carry

    lax.fori_loop(0, (n_live + UNROLL - 1) // UNROLL, group, 0)


def unpack_kernel(capacity, target, returned, out):
    def take(i, carry):
        d = target[i] // capacity
        j = target[i] % capacity
        out[i, 0:1, :] = returned[d, pl.ds(j, 1), :]
        out[i, 1:2, :] = returned[d, pl.ds(capacity + j, 1), :]
        return carry

    lax.fori_loop(0, out.shape[0], take, 0, unroll=4)


def shards(block_owner, block_band, block_count, cells, offsets, charges):
    plane_count = lax.axis_size("pln")
    pen_count = lax.axis_size("pen")
    devices = plane_count * pen_count
    local_blocks, block_len = charges.shape
    capacity = max(2, 2 * local_blocks // devices)
    total = devices * capacity
    rows = NG // pen_count
    tall = round_up(5 * capacity, 8)
    tall_back = round_up(2 * capacity, 8)
    smem = pl.BlockSpec(memory_space=pltpu.SMEM)
    vmem = pl.BlockSpec(memory_space=pltpu.VMEM)
    far = pl.BlockSpec(memory_space=pltpu.HBM)
    params = pltpu.CompilerParams(vmem_limit_bytes=VMEM_LIMIT)
    packed, target = pl.pallas_call(
        functools.partial(pack_kernel, capacity),
        out_shape=(
            jax.ShapeDtypeStruct((devices, tall, LANES), jnp.float32),
            jax.ShapeDtypeStruct((local_blocks,), jnp.int32),
        ),
        in_specs=[far] * 6,
        out_specs=(vmem, smem),
        scratch_shapes=[pltpu.SMEM((local_blocks,), jnp.int32)] * 3
        + [
            pltpu.VMEM(cells.shape, jnp.int32),
            pltpu.VMEM(offsets.shape, jnp.float32),
            pltpu.VMEM(charges.shape, jnp.float32),
            pltpu.SMEM((devices,), jnp.int32),
            pltpu.SemaphoreType.DMA((6,)),
        ],
        compiler_params=params,
        name="pack",
    )(block_owner[:, 0], block_band, block_count, cells, offsets, charges)
    received = exchange(packed, plane_count, pen_count, 0)
    bands = received[:, 4 * capacity : 5 * capacity, 0].reshape(total).astype(jnp.int32)
    table_high, table_low = (jnp.asarray(t) for t in hartley_tables())
    lines = jnp.asarray(line_tables(pen_count))
    table_scratch = [
        pltpu.VMEM((NG, NG), jnp.bfloat16),
        pltpu.VMEM((NG, NG), jnp.bfloat16),
        pltpu.VMEM(lines.shape, jnp.float32),
        pltpu.SemaphoreType.DMA((3,)),
    ]
    spectrum, edges = pl.pallas_call(
        functools.partial(deposit_kernel, capacity, rows),
        out_shape=(
            jax.ShapeDtypeStruct((rows, NG), jnp.float32),
            jax.ShapeDtypeStruct((8, NG), jnp.float32),
        ),
        in_specs=[smem, vmem] + [far] * 3,
        out_specs=(vmem, vmem),
        scratch_shapes=[
            pltpu.SMEM((total + 8,), jnp.int32),
            pltpu.VMEM((rows + 8, NG), jnp.float32),
            pltpu.VMEM((rows + 8, NG), jnp.bfloat16),
            pltpu.VMEM((rows + 8, NG), jnp.bfloat16),
        ]
        + table_scratch,
        compiler_params=params,
        name="deposit",
    )(bands, received, table_high, table_low, lines)
    gathered = share(edges, pen_count, 1)
    place = lax.axis_index("pen").astype(jnp.int32).reshape(1)
    potential, slot_forces = pl.pallas_call(
        functools.partial(solve_kernel, capacity, rows),
        out_shape=(
            jax.ShapeDtypeStruct((rows, NG), jnp.float32),
            jax.ShapeDtypeStruct((devices, tall_back, LANES), jnp.float32),
        ),
        in_specs=[smem] * 2 + [vmem] * 3 + [far] * 3,
        out_specs=(vmem, vmem),
        scratch_shapes=[
            pltpu.SMEM((total + 8,), jnp.int32),
            pltpu.VMEM((rows + 16, NG), jnp.float32),
            pltpu.VMEM((rows + 16, NG), jnp.bfloat16),
            pltpu.VMEM((rows + 16, NG), jnp.bfloat16),
            pltpu.VMEM((rows // 8, 24, NG), jnp.float32),
        ]
        + table_scratch,
        compiler_params=params,
        name="solve",
    )(bands, place, received, spectrum, gathered, table_high, table_low, lines)
    returned = exchange(slot_forces, plane_count, pen_count, 2)
    forces = pl.pallas_call(
        functools.partial(unpack_kernel, capacity),
        out_shape=jax.ShapeDtypeStruct((local_blocks, 2, block_len), jnp.float32),
        in_specs=[smem, vmem],
        out_specs=vmem,
        compiler_params=params,
        name="unpack",
    )(target, returned)
    return (potential[None], forces)


def solution(mesh):
    placed = (
        P(("pln", "pen"), None),
        P(("pln", "pen")),
        P(("pln", "pen")),
        P(("pln", "pen"), None),
        P(("pln", "pen"), None, None),
        P(("pln", "pen"), None),
    )
    return jax.shard_map(
        shards,
        mesh=mesh,
        in_specs=placed,
        out_specs=(P("pln", "pen", None), P(("pln", "pen"), None, None)),
        check_vma=False,
    )
```

profile of v0, /device:TPU:0, one launch (start us, length us, event | category | flops | bytes accessed | tf_op | source)
XLA Modules:
  0.0 125.9 jit_solution(14527568030379114422)
XLA Ops:
  0.6 0.0 copy-start.12
  0.6 0.9 copy-done.12
  1.5 0.0 copy-start.13
  1.5 0.8 copy-done.13
  2.4 0.0 copy-start.14
  2.4 0.8 copy-done.14
  3.2 0.0 copy-start.16
  3.2 0.7 copy-done.16
  3.9 0.0 copy-start.17
  3.9 0.7 copy-done.17
  4.5 0.0 copy-start.18
  4.5 0.7 copy-done.18
  5.2 2.4 %pack.1 = (f32[32,40,128]{2,1,0:T(8,128)S(1)}, s32[128]{0:T(128)S(1)}) custom-call(s32[128]{0:T(128)S(1)} %bitcast.3, s32[128]{0:T(128)S(1)} %copy-done.17, s32[128]{0:T(128)S(1)} %copy-done.18, s32[128,128]{1,0:T(8,128)S(1)} %copy-done.13, f32[128,2,128]{2,1,0:T(2,128)S(1)} %copy-done.12, f32[128,128]{1,0:T(8,128)S(1)} %copy-done.14), custom_call_target="tpu_custom_call" | custom-call | tf_op jit(solution)/shard_map/pack/pallas_call | solution.py:520
  7.6 0.0 copy-start.9
  7.6 0.8 copy-done.9
  8.5 23.1 %exchange.2.recv = f32[32,40,128]{2,1,0:T(8,128)} custom-call(f32[32,40,128]{2,1,0:T(8,128)} %copy-done.9), custom_call_target="tpu_custom_call" | custom-call | tf_op jit(solution)/shard_map/exchange/pallas_call | solution.py:165
  31.6 1.5 %convert_reduce_fusion = s32[32,8]{1,0:T(8,128)S(1)} fusion(f32[32,40,128]{2,1,0:T(8,128)} %exchange.2.recv), kind=kLoop, calls=%fused_computation | loop fusion | flops 256 | bytes 2048 | tf_op jit(solution)/shard_map/convert_element_type | solution.py:540
  33.1 0.1 convert_element_type.6.bands
  33.2 0.0 copy-start
  33.2 1.6 %copy-done = bf16[1024,1024]{1,0:T(8,128)(2,1)S(1)} copy-done((bf16[1024,1024]{1,0:T(8,128)(2,1)S(1)}, bf16[1024,1024]{1,0:T(8,128)(2,1)}, u32[]{:S(2)}) %copy-start) | copy-done | bytes 2097176
  34.8 0.0 copy-start.2
  34.8 1.1 copy-done.2
  35.9 0.0 copy-start.4
  35.9 1.0 copy-done.4
  36.9 0.0 copy-start.1
  36.9 0.0 copy-start.3
  36.9 0.0 copy-start.5
  36.9 11.9 %deposit.1 = (f32[256,1024]{1,0:T(8,128)S(1)}, f32[8,1024]{1,0:T(8,128)S(1)}) custom-call(s32[256]{0:T(256)S(1)} %convert_element_type.6.bands, f32[32,40,128]{2,1,0:T(8,128)S(1)} %copy-done.2, bf16[1024,1024]{1,0:T(8,128)(2,1)S(1)} %copy-done, bf16[1024,1024]{1,0:T(8,128)(2,1)} %constant.11.clone.table_low_h, f32[120,1024]{1,0:T(8,128)S(1)} %copy-done.4), custom_call_target="tpu_custom_call" | custom-call | tf_op jit(solution)/shard_map/deposit/pallas_call | solution.py:549
  48.8 0.0 copy-start.7
  48.8 1.0 copy-done.7
  49.8 0.0 copy-start.15
  49.8 0.6 copy-done.15
  50.4 18.0 %share.1.gathered = f32[4,8,1024]{2,1,0:T(8,128)} custom-call(f32[8,1024]{1,0:T(8,128)} %copy-done.15), custom_call_target="tpu_custom_call" | custom-call | tf_op jit(solution)/shard_map/share/pallas_call | solution.py:218
  68.4 0.0 copy-done.1
  68.4 0.0 copy-done.3
  68.4 0.0 copy-done.5
  68.4 0.0 copy-start.8
  68.5 1.2 copy-done.8
  69.7 0.0 copy-start.10
  69.7 0.9 copy-done.10
  70.6 22.0 %solve.1 = (f32[256,1024]{1,0:T(8,128)}, f32[32,16,128]{2,1,0:T(8,128)S(1)}) custom-call(s32[256]{0:T(256)S(1)} %convert_element_type.6.bands, s32[1]{0:T(128)} %bitcast.1.place, f32[32,40,128]{2,1,0:T(8,128)S(1)} %copy-done.3, f32[256,1024]{1,0:T(8,128)S(1)} %copy-done.8, f32[4,8,1024]{2,1,0:T(8,128)S(1)} %copy-done.10, bf16[1024,1024]{1,0:T(8,128)(2,1)S(1)} %copy-done.1, ...), custom_call_target="tpu_custom_call" | custom-call | tf_op jit(solution)/shard_map/solve/pallas_call | solution.py:569
  92.6 0.0 copy-start.11
  92.6 0.7 copy-done.11
  93.3 29.5 %exchange.3.returned = f32[32,16,128]{2,1,0:T(8,128)} custom-call(f32[32,16,128]{2,1,0:T(8,128)} %copy-done.11), custom_call_target="tpu_custom_call" | custom-call | tf_op jit(solution)/shard_map/exchange/pallas_call | solution.py:165
  122.8 0.0 copy-start.6
  122.8 0.9 copy-done.6
  123.7 2.1 %unpack.1 = f32[128,2,128]{2,1,0:T(2,128)} custom-call(s32[128]{0:T(128)S(1)} %get-tuple-element.12.target, f32[32,16,128]{2,1,0:T(8,128)S(1)} %copy-done.6), custom_call_target="tpu_custom_call" | custom-call | tf_op jit(solution)/shard_map/unpack/pallas_call | solution.py:589
Async XLA Ops:
  0.6 0.9 copy-start.12
  1.5 0.8 copy-start.13
  2.4 0.8 copy-start.14
  3.2 0.7 copy-start.16
  3.9 0.7 copy-start.17
  4.5 0.7 copy-start.18
  7.6 0.8 copy-start.9
  33.2 1.6 %copy-start = (bf16[1024,1024]{1,0:T(8,128)(2,1)S(1)}, bf16[1024,1024]{1,0:T(8,128)(2,1)}, u32[]{:S(2)}) copy-start(bf16[1024,1024]{1,0:T(8,128)(2,1)} %constant.10.clone.table_high_h) | copy-start | bytes 6291460
  34.8 1.1 copy-start.2
  35.9 1.0 copy-start.4
  36.9 31.5 %copy-start.1 = (bf16[1024,1024]{1,0:T(8,128)(2,1)S(1)}, bf16[1024,1024]{1,0:T(8,128)(2,1)}, u32[]{:S(2)}) copy-start(bf16[1024,1024]{1,0:T(8,128)(2,1)} %constant.10.clone.table_high_h) | copy-start | bytes 6291460
  36.9 31.5 %copy-start.3 = (f32[32,40,128]{2,1,0:T(8,128)S(1)}, f32[32,40,128]{2,1,0:T(8,128)}, u32[]{:S(2)}) copy-start(f32[32,40,128]{2,1,0:T(8,128)} %exchange.2.recv) | copy-start | bytes 1966084
  36.9 31.5 %copy-start.5 = (f32[120,1024]{1,0:T(8,128)S(1)}, f32[120,1024]{1,0:T(8,128)}, u32[]{:S(2)}) copy-start(f32[120,1024]{1,0:T(8,128)} %constant.12.clone.lines_h) | copy-start | bytes 1474564
  48.8 1.0 copy-start.7
  49.8 0.6 copy-start.15
  68.4 1.2 copy-start.8
  69.7 0.9 copy-start.10
  92.6 0.7 copy-start.11
  122.8 1.0 copy-start.6
where the time goes:
time: 126 us
  Pallas kernels  109 us (87%)
  local copies, waits for them, and re-layouts  14.5 us (12%)
  other arithmetic  1.52 us (1%)
    pallas_call x2, Pallas kernels, exchange(): pl.pallas_call(functools.partial(exchange_kernel, planes, pens), out_shap...  52.6 us
    pallas_call x1, Pallas kernels, shards(): pl.pallas_call(functools.partial(solve_kernel, capacity, rows), out_shape...  22 us
    pallas_call x1, Pallas kernels, share(): pl.pallas_call(functools.partial(share_kernel, pens), out_shape=jax.Shape...  18 us
    unnamed x38, local copies, waits for them, and re-layouts  14.4 us
    pallas_call x1, Pallas kernels, shards(): pl.pallas_call(functools.partial(deposit_kernel, capacity, rows), out_sha...  11.9 us

commit v1 on v0

--- a/solution.py
+++ b/solution.py
@@ -13,7 +13,7 @@
 LANES = 128
 CHUNKS = NG // LANES
 screening = 2e-05
-VMEM_LIMIT = 48 * 1024 * 1024
+VMEM_LIMIT = 62 * 1024 * 1024
 UNROLL = 4
 
 
@@ -72,7 +72,7 @@
     return copies
 
 
-def pack_kernel(capacity, owner_h, band_h, count_h, cells_h, offsets_h, charges_h, out, target,
+def pack_kernel(capacity, owner_h, band_h, count_h, cells_h, offsets_h, charges_h, out, header, target,
                 owner, band, count, cells, offsets, charges, used, sems):
     devices = out.shape[0]
     copies = fetch(
@@ -80,9 +80,8 @@
         (owner, band, count, cells, offsets, charges),
         sems,
     )
-    empty = 4 * capacity
-    out[...] = jnp.full(out.shape, -1.0, jnp.float32)
-    out[:, 0:empty, :] = jnp.zeros((devices, empty, LANES), jnp.float32)
+    out[...] = jnp.zeros(out.shape, jnp.float32)
+    header[...] = jnp.full(header.shape, -1, jnp.int32)
 
     def clear(i, carry):
         used[i] = 0
@@ -103,7 +102,7 @@
         out[o, pl.ds(capacity + j, 1), :] = pair[1:2]
         out[o, pl.ds(2 * capacity + j, 1), :] = jnp.where(lane < count[i], charges[pl.ds(i, 1), :], 0.0)
         out[o, pl.ds(3 * capacity + j, 1), :] = cells[pl.ds(i, 1), :].astype(jnp.float32)
-        out[o, pl.ds(4 * capacity + j, 1), :] = jnp.full((1, LANES), band[i], jnp.int32).astype(jnp.float32)
+        header[o] = jnp.where(lane == j, band[i], header[o])
         return carry
 
     lax.fori_loop(0, owner.shape[0], place, 0)
@@ -113,7 +112,9 @@
     return (lax.div(index, pens), lax.rem(index, pens))
 
 
-def exchange_kernel(planes, pens, source, target, send_sems, recv_sems, own_sem):
+def exchange_kernel(planes, pens, arrays, *refs):
+    sources, targets = refs[:arrays], refs[arrays : 2 * arrays]
+    send_sems, recv_sems, own_sems = refs[2 * arrays :]
     count = planes * pens
     me = lax.axis_index("pln") * pens + lax.axis_index("pen")
     barrier = pltpu.get_barrier_semaphore()
@@ -123,58 +124,62 @@
         pl.semaphore_signal(barrier, inc=1, device_id=other, device_id_type=pl.DeviceIdType.MESH)
         return carry
 
-    own = pltpu.make_async_copy(source.at[me], target.at[me], own_sem)
-    own.start()
+    own = [
+        pltpu.make_async_copy(sources[n].at[me], targets[n].at[me], own_sems.at[n]) for n in range(arrays)
+    ]
+    for copy in own:
+        copy.start()
     lax.fori_loop(1, count, greet, 0)
     pl.semaphore_wait(barrier, count - 1)
 
-    def copy_to(k):
-        to = lax.rem(me + k, count)
+    def copy_of(n, k, source, target, other):
         return pltpu.make_async_remote_copy(
-            src_ref=source.at[to],
-            dst_ref=target.at[me],
-            send_sem=send_sems.at[k],
-            recv_sem=recv_sems.at[k],
-            device_id=peer(to, pens),
+            src_ref=sources[n].at[source],
+            dst_ref=targets[n].at[target],
+            send_sem=send_sems.at[n, k],
+            recv_sem=recv_sems.at[n, k],
+            device_id=peer(other, pens),
             device_id_type=pl.DeviceIdType.MESH,
         )
 
     def send(k, carry):
-        copy_to(k).start()
+        to = lax.rem(me + k, count)
+        for n in range(arrays):
+            copy_of(n, k, to, me, to).start()
         return carry
 
     def finish(k, carry):
-        copy_to(k).wait_send()
-        pltpu.make_async_remote_copy(
-            src_ref=source.at[me],
-            dst_ref=target.at[lax.rem(me - k + count, count)],
-            send_sem=send_sems.at[k],
-            recv_sem=recv_sems.at[k],
-            device_id=peer(lax.rem(me - k + count, count), pens),
-            device_id_type=pl.DeviceIdType.MESH,
-        ).wait_recv()
+        to = lax.rem(me + k, count)
+        behind = lax.rem(me - k + count, count)
+        for n in range(arrays):
+            copy_of(n, k, to, me, to).wait_send()
+            copy_of(n, k, me, behind, behind).wait_recv()
         return carry
 
     lax.fori_loop(1, count, send, 0)
     lax.fori_loop(1, count, finish, 0)
-    own.wait()
+    for copy in own:
+        copy.wait()
 
 
 def exchange(values, planes, pens, number):
     place = pl.BlockSpec(memory_space=pl.ANY)
+    arrays = len(values)
     return pl.pallas_call(
-        functools.partial(exchange_kernel, planes, pens),
-        out_shape=jax.ShapeDtypeStruct(values.shape, values.dtype),
-        in_specs=[place],
-        out_specs=place,
+        functools.partial(exchange_kernel, planes, pens, arrays),
+        out_shape=tuple(jax.ShapeDtypeStruct(v.shape, v.dtype) for v in values),
+        in_specs=[place] * arrays,
+        out_specs=(place,) * arrays,
         scratch_shapes=[
-            pltpu.SemaphoreType.DMA((planes * pens,)),
-            pltpu.SemaphoreType.DMA((planes * pens,)),
-            pltpu.SemaphoreType.DMA,
+            pltpu.SemaphoreType.DMA((arrays, planes * pens)),
+            pltpu.SemaphoreType.DMA((arrays, planes * pens)),
+            pltpu.SemaphoreType.DMA((arrays,)),
         ],
-        compiler_params=pltpu.CompilerParams(collective_id=number, has_side_effects=True),
+        compiler_params=pltpu.CompilerParams(
+            collective_id=number, has_side_effects=True, vmem_limit_bytes=VMEM_LIMIT
+        ),
         name="exchange",
-    )(values)
+    )(*values)
 
 
 def share_kernel(pens, source, target, send_sems, recv_sems, own_sem):
@@ -225,31 +230,35 @@
             pltpu.SemaphoreType.DMA((pens,)),
             pltpu.SemaphoreType.DMA,
         ],
-        compiler_params=pltpu.CompilerParams(collective_id=number, has_side_effects=True),
+        compiler_params=pltpu.CompilerParams(collective_id=number, has_side_effects=True, vmem_limit_bytes=VMEM_LIMIT),
         name="share",
     )(values)
 
 
-def live_list(bands, live, capacity):
-    total = bands.shape[0]
-
-    def check(s, n):
-        live[n] = s
-        return n + jnp.where(bands[s] >= 0, 1, 0)
-
-    return lax.fori_loop(0, total, check, jnp.int32(0))
+def live_list(header, live, capacity):
+    def check(d, n):
+        for j in range(capacity):
+            live[n] = d * capacity + j
+            n = n + jnp.where(header[d, 0, j] >= 0, 1, 0)
+        return n
+
+    return lax.fori_loop(0, header.shape[0], check, jnp.int32(0))
 
 
 def particle(recv, capacity, s):
     d = s // capacity
     j = s % capacity
-    frac_x = recv[d, pl.ds(j, 1), :]
-    frac_y = recv[d, pl.ds(capacity + j, 1), :]
-    weight = recv[d, pl.ds(2 * capacity + j, 1), :]
-    cell = recv[d, pl.ds(3 * capacity + j, 1), :].astype(jnp.int32)
-    column = cell % NG
-    after = (column + 1) % NG
-    row = cell // NG
+
+    def spread(which):
+        return recv[d, pl.ds(which * capacity + j, 8, stride=0), :]
+
+    frac_x = spread(0)
+    frac_y = spread(1)
+    weight = spread(2)
+    cell = spread(3).astype(jnp.int32)
+    column = cell & (NG - 1)
+    after = (column + 1) & (NG - 1)
+    row = cell >> (NG.bit_length() - 1)
     left = (1.0 - frac_x).astype(jnp.bfloat16).astype(jnp.float32)
     right = frac_x.astype(jnp.bfloat16).astype(jnp.float32)
     return frac_y, weight, row, column, after, left, right
@@ -265,14 +274,20 @@
     return high, (values - high.astype(jnp.float32)).astype(jnp.bfloat16)
 
 
-def deposit_kernel(capacity, rows, bands, recv, table_high_h, table_low_h, lines_h, spectrum, edges,
-                   live, dens, hi, lo, table_high, table_low, lines, sems):
-    total = bands.shape[0]
-    copies = fetch((table_high_h, table_low_h, lines_h), (table_high, table_low, lines), sems)
-    n_live = live_list(bands, live, capacity)
+def deposit_kernel(capacity, rows, header_h, recv_h, table_high_h, table_low_h, lines_h, spectrum, edges,
+                   live, dens, hi, lo, tails, header, recv, table_high, table_low, lines, sems):
+    copies = fetch(
+        (header_h, recv_h, table_high_h, table_low_h, lines_h),
+        (header, recv.at[:, 0 : 4 * capacity], table_high, table_low, lines),
+        sems,
+    )
     dens[...] = jnp.zeros(dens.shape, jnp.float32)
+    tails[...] = jnp.zeros(tails.shape, jnp.float32)
+    copies[0].wait()
+    n_live = live_list(header, live, capacity)
+    copies[1].wait()
     sub8 = lax.broadcasted_iota(jnp.int32, (8, LANES), 0)
-    sub_all = lax.broadcasted_iota(jnp.int32, (LANES, LANES), 0)
+    places = [sub8 + 8 * b for b in range(LANES // 8)]
 
     def one(slot_at):
         alive = slot_at < n_live
@@ -282,34 +297,45 @@
         lower = (weight * (1.0 - frac_y)).astype(jnp.bfloat16).astype(jnp.float32)
         upper = (weight * frac_y).astype(jnp.bfloat16).astype(jnp.float32)
         main = jnp.where(row == sub8, lower, jnp.where(row + 1 == sub8, upper, 0.0))
-        tail = jnp.where((sub8 == 0) & (row == 7), upper, 0.0)
-        tall = jnp.concatenate([main, tail], axis=0)
-        chunk = column // LANES
-        chunk_after = after // LANES
-        row_left = jnp.concatenate([jnp.where(chunk == a, tall, 0.0) for a in range(CHUNKS)], axis=0)
-        row_right = jnp.concatenate([jnp.where(chunk_after == a, tall, 0.0) for a in range(CHUNKS)], axis=0)
-        col_left = jnp.where(column % LANES == sub_all, left, 0.0)
-        col_right = jnp.where(after % LANES == sub_all, right, 0.0)
-        lhs = jnp.concatenate([row_left.astype(jnp.bfloat16), row_right.astype(jnp.bfloat16)], axis=1)
-        rhs = jnp.concatenate([col_left.astype(jnp.bfloat16), col_right.astype(jnp.bfloat16)], axis=1)
+        tail = jnp.where(row == 7, upper, 0.0)
+
+        def row_side(chunk):
+            tiles = [jnp.where(chunk == a, main, 0.0) for a in range(CHUNKS)]
+            tiles += [jnp.where(chunk == sub8, tail, 0.0), jnp.zeros((8, LANES), jnp.float32)]
+            return jnp.concatenate(tiles, axis=0).astype(jnp.bfloat16)
+
+        def column_side(lane, factor):
+            return jnp.concatenate([jnp.where(lane == b, factor, 0.0) for b in places], axis=0).astype(jnp.bfloat16)
+
+        lhs = jnp.concatenate([row_side(column >> 7), row_side(after >> 7)], axis=1)
+        rhs = jnp.concatenate([column_side(column & 127, left), column_side(after & 127, right)], axis=1)
         values = lax.dot_general(lhs, rhs, (((1,), (1,)), ((), ())), preferred_element_type=jnp.float32)
-        return jnp.maximum(bands[s], 0), values
+        return jnp.maximum(header[s // capacity, 0, s % capacity], 0), values
 
     def group(g, carry):
         results = [one(g * UNROLL + k) for k in range(UNROLL)]
         for band, values in results:
             start = pl.multiple_of(band * 8, 8)
             for a in range(CHUNKS):
-                lanes = slice(a * LANES, (a + 1) * LANES)
-                dens[pl.ds(start, 16), lanes] += values[a * 16 : (a + 1) * 16]
+                dens[pl.ds(start, 8), a * LANES : (a + 1) * LANES] += values[a * 8 : (a + 1) * 8]
+            tails[band] += values[CHUNKS * 8 : CHUNKS * 8 + 8]
         return carry
 
     lax.fori_loop(0, (n_live + UNROLL - 1) // UNROLL, group, 0)
+
+    def carry_row(t, carry):
+        start = pl.multiple_of(t * 8 + 8, 8)
+        extra = tails[t]
+        for a in range(CHUNKS):
+            dens[pl.ds(start, 1), a * LANES : (a + 1) * LANES] += extra[a : a + 1]
+        return carry
+
+    lax.fori_loop(0, rows // 8, carry_row, 0)
     high, low = split(dens[...])
     hi[...] = high
     lo[...] = low
     width = 256
-    for copy in copies:
+    for copy in copies[2:]:
         copy.wait()
     for n in range(NG // width):
         cols = slice(n * width, (n + 1) * width)
@@ -334,10 +360,15 @@
     edges[6:8] = jnp.zeros((2, NG), jnp.float32)
 
 
-def solve_kernel(capacity, rows, bands, place, recv, spectrum, gathered, table_high_h, table_low_h, lines_h, potential, forces,
-                 live, wave, hi, lo, field, table_high, table_low, lines, sems):
-    copies = fetch((lines_h, table_high_h, table_low_h), (lines, table_high, table_low), sems)
-    copies[0].wait()
+def solve_kernel(capacity, rows, place, header_h, recv_h, spectrum_h, gathered_h, table_high_h, table_low_h, lines_h, potential_h, forces,
+                 live, wave, hi, lo, field, rim, potential, spectrum, gathered, header, recv, table_high, table_low, lines, sems):
+    copies = fetch(
+        (lines_h, gathered_h, spectrum_h, table_high_h, table_low_h, header_h, recv_h),
+        (lines, gathered, spectrum, table_high, table_low, header, recv.at[:, 0 : 4 * capacity]),
+        sems,
+    )
+    for copy in copies[:3]:
+        copy.wait()
     pens = gathered.shape[0]
     mine = place[0]
 
@@ -410,12 +441,14 @@
     hi[...] = high
     lo[...] = low
     width = 256
-    copies[1].wait()
-    copies[2].wait()
+    for copy in copies[3:5]:
+        copy.wait()
     for n in range(NG // width):
         cols = slice(n * width, (n + 1) * width)
         wave[:, cols] = dot3(hi[...], lo[...], table_high[:, cols], table_low[:, cols])
     potential[...] = wave[8 : rows + 8]
+    out_copy = pltpu.make_async_copy(potential, potential_h, sems.at[7])
+    out_copy.start()
 
     def derive(t, carry):
         base = pl.multiple_of(t * 8, 8)
@@ -439,16 +472,17 @@
 
         @pl.when(t > 0)
         def _():
-            field[t - 1, 16:17, :] = along_x[0:1]
-            field[t - 1, 17:18, :] = along_y[0:1]
+            for a in range(CHUNKS):
+                lanes = slice(a * LANES, (a + 1) * LANES)
+                rim[t - 1, 2 * a : 2 * a + 1, :] = along_x[0:1, lanes]
+                rim[t - 1, 2 * a + 1 : 2 * a + 2, :] = along_y[0:1, lanes]
 
         return carry
 
     lax.fori_loop(0, tiles + 1, derive, 0)
-    for t in range(tiles):
-        field[t, 18:24, :] = jnp.zeros((6, NG), jnp.float32)
-
-    n_live = live_list(bands, live, capacity)
+    for copy in copies[5:]:
+        copy.wait()
+    n_live = live_list(header, live, capacity)
     forces[...] = jnp.zeros(forces.shape, jnp.float32)
     sub8 = lax.broadcasted_iota(jnp.int32, (8, LANES), 0)
 
@@ -457,26 +491,36 @@
 
     def one(slot_at):
         s = live[jnp.minimum(slot_at, n_live - 1)]
-        band = bands[s]
+        band = header[s // capacity, 0, s % capacity]
         frac_y, weight, row, column, after, left, right = particle(recv, capacity, s)
-        index = jnp.broadcast_to(column % LANES, (8, LANES))
-        index_after = jnp.broadcast_to(after % LANES, (8, LANES))
-        chunk = jnp.broadcast_to(column // LANES, (8, LANES))
-        chunk_after = jnp.broadcast_to(after // LANES, (8, LANES))
+        index = column & 127
+        index_after = after & 127
+        chunk = column >> 7
+        chunk_after = after >> 7
+        here = [chunk == a for a in range(1, CHUNKS)]
+        there = [chunk_after == a for a in range(1, CHUNKS)]
+        row_weight = weight * jnp.where(row == sub8, 1.0 - frac_y, jnp.where(row + 1 == sub8, frac_y, 0.0))
         mixed = []
-        for part in range(3):
-            near = jnp.zeros((8, LANES), jnp.float32)
-            far = near
+        for part in range(2):
             for a in range(CHUNKS):
                 values = field[band, part * 8 : part * 8 + 8, a * LANES : (a + 1) * LANES]
-                near = jnp.where(chunk == a, pick(values, index), near)
-                far = jnp.where(chunk_after == a, pick(values, index_after), far)
-            mixed.append(left * near + right * far)
-        row_weight = jnp.where(row == sub8, 1.0 - frac_y, jnp.where(row + 1 == sub8, frac_y, 0.0))
-        edge = jnp.where(row == 7, frac_y, 0.0)
+                g, h = pick(values, index), pick(values, index_after)
+                near = g if a == 0 else jnp.where(here[a - 1], g, near)
+                far = h if a == 0 else jnp.where(there[a - 1], h, far)
+            mixed.append(row_weight * (left * near + right * far))
+        edge = weight * jnp.where(row == 7, frac_y, 0.0)
+        pair = sub8 >> 1
+        rims = jnp.zeros((8, LANES), jnp.float32)
+        for half in range(2):
+            values = rim[band, half * 8 : half * 8 + 8, :]
+            spot = pair + half * 4
+            rims += jnp.where(spot == chunk, left * pick(values, index), 0.0)
+            rims += jnp.where(spot == chunk_after, right * pick(values, index_after), 0.0)
+        rims = edge * rims
+        odd = (sub8 & 1) == 1
         out = [
-            weight * (jnp.sum(row_weight * mixed[c], axis=0, keepdims=True) + edge * mixed[2][c : c + 1])
-            for c in range(2)
+            jnp.sum(mixed[0] + jnp.where(odd, 0.0, rims), axis=0, keepdims=True),
+            jnp.sum(mixed[1] + jnp.where(odd, rims, 0.0), axis=0, keepdims=True),
         ]
         return s, out
 
@@ -490,6 +534,7 @@
         return carry
 
     lax.fori_loop(0, (n_live + UNROLL - 1) // UNROLL, group, 0)
+    out_copy.wait()
 
 
 def unpack_kernel(capacity, target, returned, out):
@@ -511,20 +556,21 @@
     capacity = max(2, 2 * local_blocks // devices)
     total = devices * capacity
     rows = NG // pen_count
-    tall = round_up(5 * capacity, 8)
+    tall = 4 * capacity
     tall_back = round_up(2 * capacity, 8)
     smem = pl.BlockSpec(memory_space=pltpu.SMEM)
     vmem = pl.BlockSpec(memory_space=pltpu.VMEM)
     far = pl.BlockSpec(memory_space=pltpu.HBM)
     params = pltpu.CompilerParams(vmem_limit_bytes=VMEM_LIMIT)
-    packed, target = pl.pallas_call(
+    packed, header, target = pl.pallas_call(
         functools.partial(pack_kernel, capacity),
         out_shape=(
             jax.ShapeDtypeStruct((devices, tall, LANES), jnp.float32),
+            jax.ShapeDtypeStruct((devices, 1, LANES), jnp.int32),
             jax.ShapeDtypeStruct((local_blocks,), jnp.int32),
         ),
         in_specs=[far] * 6,
-        out_specs=(vmem, smem),
+        out_specs=(vmem, vmem, smem),
         scratch_shapes=[pltpu.SMEM((local_blocks,), jnp.int32)] * 3
         + [
             pltpu.VMEM(cells.shape, jnp.int32),
@@ -536,15 +582,18 @@
         compiler_params=params,
         name="pack",
     )(block_owner[:, 0], block_band, block_count, cells, offsets, charges)
-    received = exchange(packed, plane_count, pen_count, 0)
-    bands = received[:, 4 * capacity : 5 * capacity, 0].reshape(total).astype(jnp.int32)
+    received, header = exchange((packed, header), plane_count, pen_count, 0)
     table_high, table_low = (jnp.asarray(t) for t in hartley_tables())
     lines = jnp.asarray(line_tables(pen_count))
+    arrived = [
+        pltpu.SMEM(header.shape, jnp.int32),
+        pltpu.VMEM((devices, tall + 8, LANES), jnp.float32),
+    ]
     table_scratch = [
         pltpu.VMEM((NG, NG), jnp.bfloat16),
         pltpu.VMEM((NG, NG), jnp.bfloat16),
         pltpu.VMEM(lines.shape, jnp.float32),
-        pltpu.SemaphoreType.DMA((3,)),
+        pltpu.SemaphoreType.DMA((8,)),
     ]
     spectrum, edges = pl.pallas_call(
         functools.partial(deposit_kernel, capacity, rows),
@@ -552,18 +601,20 @@
             jax.ShapeDtypeStruct((rows, NG), jnp.float32),
             jax.ShapeDtypeStruct((8, NG), jnp.float32),
         ),
-        in_specs=[smem, vmem] + [far] * 3,
+        in_specs=[far] * 5,
         out_specs=(vmem, vmem),
         scratch_shapes=[
             pltpu.SMEM((total + 8,), jnp.int32),
             pltpu.VMEM((rows + 8, NG), jnp.float32),
             pltpu.VMEM((rows + 8, NG), jnp.bfloat16),
             pltpu.VMEM((rows + 8, NG), jnp.bfloat16),
+            pltpu.VMEM((rows // 8, 8, LANES), jnp.float32),
         ]
+        + arrived
         + table_scratch,
         compiler_params=params,
         name="deposit",
-    )(bands, received, table_high, table_low, lines)
+    )(header, received, table_high, table_low, lines)
     gathered = share(edges, pen_count, 1)
     place = lax.axis_index("pen").astype(jnp.int32).reshape(1)
     potential, slot_forces = pl.pallas_call(
@@ -572,20 +623,25 @@
             jax.ShapeDtypeStruct((rows, NG), jnp.float32),
             jax.ShapeDtypeStruct((devices, tall_back, LANES), jnp.float32),
         ),
-        in_specs=[smem] * 2 + [vmem] * 3 + [far] * 3,
-        out_specs=(vmem, vmem),
+        in_specs=[smem] + [far] * 7,
+        out_specs=(far, vmem),
         scratch_shapes=[
             pltpu.SMEM((total + 8,), jnp.int32),
             pltpu.VMEM((rows + 16, NG), jnp.float32),
             pltpu.VMEM((rows + 16, NG), jnp.bfloat16),
             pltpu.VMEM((rows + 16, NG), jnp.bfloat16),
-            pltpu.VMEM((rows // 8, 24, NG), jnp.float32),
+            pltpu.VMEM((rows // 8, 16, NG), jnp.float32),
+            pltpu.VMEM((rows // 8, 16, LANES), jnp.float32),
+            pltpu.VMEM((rows, NG), jnp.float32),
+            pltpu.VMEM((rows, NG), jnp.float32),
+            pltpu.VMEM(gathered.shape, jnp.float32),
         ]
+        + arrived
         + table_scratch,
         compiler_params=params,
         name="solve",
-    )(bands, place, received, spectrum, gathered, table_high, table_low, lines)
-    returned = exchange(slot_forces, plane_count, pen_count, 2)
+    )(place, header, received, spectrum, gathered, table_high, table_low, lines)
+    (returned,) = exchange((slot_forces,), plane_count, pen_count, 2)
     forces = pl.pallas_call(
         functools.partial(unpack_kernel, capacity),
         out_shape=jax.ShapeDtypeStruct((local_blocks, 2, block_len), jnp.float32),

time: 126 us -> 100 us (0.79)
  local copies, waits for them, and re-layouts: 14.5 us -> 0 us
  Pallas kernels: 109 us -> 99.2 us
  other arithmetic: 1.52 us -> 0 us
    pallas_call x2, Pallas kernels: 52.6 us -> 33.5 us  [exchange(): pl.pallas_call(functools.partial(exchange_kernel, planes, pens, arrays),...]
    unnamed x38 -> x0, local copies, waits for them, and re-layouts: 14.4 us -> none
    pallas_call x1, Pallas kernels: 18 us -> 7.25 us  [share(): pl.pallas_call(functools.partial(share_kernel, pens), out_shape=jax.Shape...]
    pallas_call x1, Pallas kernels: 22 us -> 32.7 us  [shards(): pl.pallas_call(functools.partial(solve_kernel, capacity, rows), out_shape...]
    pallas_call x1, Pallas kernels: 11.9 us -> 20.2 us  [shards(): pl.pallas_call(functools.partial(deposit_kernel, capacity, rows), out_sha...]
    convert_element_type x1 -> x0, other arithmetic: 1.52 us -> none  [shards(): received[:, 4 * capacity:5 * capacity, 0].reshape(total).astype(jnp.int32)]
where the time goes in v1:
time: 100 us; the launch traced here: 99.9 us
  Pallas kernels  99.2 us (99%)
    pallas_call x2, Pallas kernels, exchange(): pl.pallas_call(functools.partial(exchange_kernel, planes, pens, arrays),...  33.5 us
    pallas_call x1, Pallas kernels, shards(): pl.pallas_call(functools.partial(solve_kernel, capacity, rows), out_shape...  32.7 us
    pallas_call x1, Pallas kernels, shards(): pl.pallas_call(functools.partial(deposit_kernel, capacity, rows), out_sha...  20.2 us
    pallas_call x1, Pallas kernels, share(): pl.pallas_call(functools.partial(share_kernel, pens), out_shape=jax.Shape...  7.25 us
    pallas_call x1, Pallas kernels, shards(): pl.pallas_call(functools.partial(pack_kernel, capacity), out_shape=(jax.S...  3.01 us
    pallas_call x1, Pallas kernels, shards(): pl.pallas_call(functools.partial(unpack_kernel, capacity), out_shape=jax....  2.56 us

profile of v1, /device:TPU:0, one launch (start us, length us, event | category | flops | bytes accessed | tf_op | source)
XLA Modules:
  0.0 99.9 jit_solution(12315670397118017429)
XLA Ops:
  0.6 3.0 %pack.1 = (f32[32,32,128]{2,1,0:T(8,128)}, s32[32,1,128]{2,1,0:T(1,128)}, s32[128]{0:T(128)}) custom-call(s32[128]{0:T(128)} %bitcast.3, s32[128]{0:T(128)} %band_h.1, s32[128]{0:T(128)} %count_h.1, s32[128,128]{1,0:T(8,128)} %cells_h.1, f32[128,2,128]{2,1,0:T(2,128)} %offsets_h.1, f32[128,128]{1,0:T(8,128)} %charges_h.1), custom_call_target="tpu_custom_call" | custom-call | tf_op jit(solution)/shard_map/pack/pallas_call | solution.py:565
  3.7 21.5 %exchange.2 = (f32[32,32,128]{2,1,0:T(8,128)}, s32[32,1,128]{2,1,0:T(1,128)}) custom-call(f32[32,32,128]{2,1,0:T(8,128)} %get-tuple-element.11.refs_0_, s32[32,1,128]{2,1,0:T(1,128)} %get-tuple-element.12.refs_1_), custom_call_target="tpu_custom_call" | custom-call | tf_op jit(solution)/shard_map/exchange/pallas_call | solution.py:168
  25.2 20.2 %deposit.1 = (f32[256,1024]{1,0:T(8,128)}, f32[8,1024]{1,0:T(8,128)}) custom-call(s32[32,1,128]{2,1,0:T(1,128)} %get-tuple-element.13.header_h, f32[32,32,128]{2,1,0:T(8,128)} %get-tuple-element.14.recv_h, bf16[1024,1024]{1,0:T(8,128)(2,1)} %constant.10.clone.table_high_h, bf16[1024,1024]{1,0:T(8,128)(2,1)} %constant.11.clone.table_low_h, ...), custom_call_target="tpu_custom_call" | custom-call | tf_op jit(solution)/shard_map/deposit/pallas_call | solution.py:598
  45.3 7.2 %share.1.gathered_h = f32[4,8,1024]{2,1,0:T(8,128)} custom-call(f32[8,1024]{1,0:T(8,128)} %get-tuple-element.16.source), custom_call_target="tpu_custom_call" | custom-call | tf_op jit(solution)/shard_map/share/pallas_call | solution.py:223
  52.6 32.7 %solve.1 = (f32[256,1024]{1,0:T(8,128)}, f32[32,16,128]{2,1,0:T(8,128)}) custom-call(s32[1]{0:T(128)} %bitcast.place, s32[32,1,128]{2,1,0:T(1,128)} %get-tuple-element.13.header_h, f32[32,32,128]{2,1,0:T(8,128)} %get-tuple-element.14.recv_h, f32[256,1024]{1,0:T(8,128)} %get-tuple-element.15.spectrum_h, f32[4,8,1024]{2,1,0:T(8,128)} %share.1.gathered_h, ...), custom_call_target="tpu_custom_call" | custom-call | tf_op jit(solution)/shard_map/solve/pallas_call | solution.py:620
  85.3 12.0 %exchange.3.returned = f32[32,16,128]{2,1,0:T(8,128)} custom-call(f32[32,16,128]{2,1,0:T(8,128)} %get-tuple-element.19.refs_0_), custom_call_target="tpu_custom_call" | custom-call | tf_op jit(solution)/shard_map/exchange/pallas_call | solution.py:168
  97.3 2.6 %unpack.1 = f32[128,2,128]{2,1,0:T(2,128)} custom-call(s32[128]{0:T(128)} %get-tuple-element.18.target, f32[32,16,128]{2,1,0:T(8,128)} %exchange.3.returned), custom_call_target="tpu_custom_call" | custom-call | tf_op jit(solution)/shard_map/unpack/pallas_call | solution.py:645

commit v2 on v1

--- a/solution.py
+++ b/solution.py
@@ -252,10 +252,11 @@
     def spread(which):
         return recv[d, pl.ds(which * capacity + j, 8, stride=0), :]
 
-    frac_x = spread(0)
-    frac_y = spread(1)
-    weight = spread(2)
-    cell = spread(3).astype(jnp.int32)
+    return factors(spread(0), spread(1), spread(2), spread(3))
+
+
+def factors(frac_x, frac_y, weight, cell):
+    cell = cell.astype(jnp.int32)
     column = cell & (NG - 1)
     after = (column + 1) & (NG - 1)
     row = cell >> (NG.bit_length() - 1)
@@ -360,11 +361,11 @@
     edges[6:8] = jnp.zeros((2, NG), jnp.float32)
 
 
-def solve_kernel(capacity, rows, place, header_h, recv_h, spectrum_h, gathered_h, table_high_h, table_low_h, lines_h, potential_h, forces,
-                 live, wave, hi, lo, field, rim, potential, spectrum, gathered, header, recv, table_high, table_low, lines, sems):
+def solve_kernel(rows, place, spectrum_h, gathered_h, table_high_h, table_low_h, lines_h, potential_h, field_h, rim,
+                 wave, hi, lo, field, potential, spectrum, gathered, table_high, table_low, lines, sems):
     copies = fetch(
-        (lines_h, gathered_h, spectrum_h, table_high_h, table_low_h, header_h, recv_h),
-        (lines, gathered, spectrum, table_high, table_low, header, recv.at[:, 0 : 4 * capacity]),
+        (lines_h, gathered_h, spectrum_h, table_high_h, table_low_h),
+        (lines, gathered, spectrum, table_high, table_low),
         sems,
     )
     for copy in copies[:3]:
@@ -469,6 +470,7 @@
         def _():
             field[t, 0:8, :] = along_x
             field[t, 8:16, :] = along_y
+            pltpu.make_async_copy(field.at[t], field_h.at[t], sems.at[6]).start()
 
         @pl.when(t > 0)
         def _():
@@ -480,19 +482,41 @@
         return carry
 
     lax.fori_loop(0, tiles + 1, derive, 0)
-    for copy in copies[5:]:
+    pltpu.make_async_copy(field, field_h, sems.at[6]).wait()
+    out_copy.wait()
+
+
+def pull_kernel(planes, pens, capacity, target, header_h, recv_h, field_h, rim_h, out,
+                forces, returned, header, recv, field, rim, sems, send_sems, recv_sems):
+    count = planes * pens
+    me = lax.axis_index("pln") * pens + lax.axis_index("pen")
+    barrier = pltpu.get_barrier_semaphore()
+    copies = fetch((field_h, header_h, recv_h, rim_h), (field, header, recv, rim), sems)
+
+    def greet(k, carry):
+        other = peer(lax.rem(me + k, count), pens)
+        pl.semaphore_signal(barrier, inc=1, device_id=other, device_id_type=pl.DeviceIdType.MESH)
+        return carry
+
+    lax.fori_loop(1, count, greet, 0)
+    for copy in copies:
         copy.wait()
-    n_live = live_list(header, live, capacity)
-    forces[...] = jnp.zeros(forces.shape, jnp.float32)
     sub8 = lax.broadcasted_iota(jnp.int32, (8, LANES), 0)
+    odd = (sub8 & 1) == 1
+    pair = sub8 >> 1
 
     def pick(values, index):
         return jnp.take_along_axis(values, index, axis=1, mode="promise_in_bounds")
 
-    def one(slot_at):
-        s = live[jnp.minimum(slot_at, n_live - 1)]
-        band = header[s // capacity, 0, s % capacity]
-        frac_y, weight, row, column, after, left, right = particle(recv, capacity, s)
+    def one(d, j):
+        def spread(which):
+            at = which * capacity + j
+            return jnp.broadcast_to(recv[d, at : at + 1, :], (8, LANES))
+
+        band = jnp.maximum(header[d, 0, j], 0)
+        frac_y, weight, row, column, after, left, right = factors(
+            spread(0), spread(1), spread(2), spread(3)
+        )
         index = column & 127
         index_after = after & 127
         chunk = column >> 7
@@ -500,44 +524,68 @@
         here = [chunk == a for a in range(1, CHUNKS)]
         there = [chunk_after == a for a in range(1, CHUNKS)]
         row_weight = weight * jnp.where(row == sub8, 1.0 - frac_y, jnp.where(row + 1 == sub8, frac_y, 0.0))
+        rows_of = field[band]
         mixed = []
         for part in range(2):
             for a in range(CHUNKS):
-                values = field[band, part * 8 : part * 8 + 8, a * LANES : (a + 1) * LANES]
+                values = rows_of[part * 8 : part * 8 + 8, a * LANES : (a + 1) * LANES]
                 g, h = pick(values, index), pick(values, index_after)
                 near = g if a == 0 else jnp.where(here[a - 1], g, near)
                 far = h if a == 0 else jnp.where(there[a - 1], h, far)
             mixed.append(row_weight * (left * near + right * far))
         edge = weight * jnp.where(row == 7, frac_y, 0.0)
-        pair = sub8 >> 1
         rims = jnp.zeros((8, LANES), jnp.float32)
+        rims_of = rim[band]
         for half in range(2):
-            values = rim[band, half * 8 : half * 8 + 8, :]
+            values = rims_of[half * 8 : half * 8 + 8]
             spot = pair + half * 4
             rims += jnp.where(spot == chunk, left * pick(values, index), 0.0)
             rims += jnp.where(spot == chunk_after, right * pick(values, index_after), 0.0)
         rims = edge * rims
-        odd = (sub8 & 1) == 1
-        out = [
+        return [
             jnp.sum(mixed[0] + jnp.where(odd, 0.0, rims), axis=0, keepdims=True),
             jnp.sum(mixed[1] + jnp.where(odd, rims, 0.0), axis=0, keepdims=True),
         ]
-        return s, out
-
-    def group(g, carry):
-        results = [one(g * UNROLL + k) for k in range(UNROLL)]
-        for s, values in results:
-            d = s // capacity
-            j = s % capacity
-            forces[d, pl.ds(j, 1), :] = values[0]
-            forces[d, pl.ds(capacity + j, 1), :] = values[1]
-        return carry
-
-    lax.fori_loop(0, (n_live + UNROLL - 1) // UNROLL, group, 0)
-    out_copy.wait()
-
-
-def unpack_kernel(capacity, target, returned, out):
+
+    def pull(d):
+        made = [one(d, j) for j in range(capacity)]
+        for c in range(2):
+            for j in range(capacity):
+                forces[d, c * capacity + j : c * capacity + j + 1, :] = made[j][c]
+        if forces.shape[1] > 2 * capacity:
+            forces[d, 2 * capacity :, :] = jnp.zeros((forces.shape[1] - 2 * capacity, LANES), jnp.float32)
+
+    def copy_of(k, source, place, other):
+        return pltpu.make_async_remote_copy(
+            src_ref=forces.at[source],
+            dst_ref=returned.at[place],
+            send_sem=send_sems.at[k],
+            recv_sem=recv_sems.at[k],
+            device_id=peer(other, pens),
+            device_id_type=pl.DeviceIdType.MESH,
+        )
+
+    pull(lax.rem(me + 1, count))
+    pl.semaphore_wait(barrier, count - 1)
+
+    def step(k, carry):
+        to = lax.rem(me + k, count)
+        copy_of(k, to, me, to).start()
+        pull(lax.rem(me + k + 1, count))
+        return carry
+
+    lax.fori_loop(1, count, step, 0)
+    returned[me] = forces[me]
+
+    def finish(k, carry):
+        to = lax.rem(me + k, count)
+        behind = lax.rem(me - k + count, count)
+        copy_of(k, to, me, to).wait_send()
+        copy_of(k, me, behind, behind).wait_recv()
+        return carry
+
+    lax.fori_loop(1, count, finish, 0)
+
     def take(i, carry):
         d = target[i] // capacity
         j = target[i] % capacity
@@ -545,7 +593,7 @@
         out[i, 1:2, :] = returned[d, pl.ds(capacity + j, 1), :]
         return carry
 
-    lax.fori_loop(0, out.shape[0], take, 0, unroll=4)
+    lax.fori_loop(0, out.shape[0], take, 0)
 
 
 def shards(block_owner, block_band, block_count, cells, offsets, charges):
@@ -617,39 +665,49 @@
     )(header, received, table_high, table_low, lines)
     gathered = share(edges, pen_count, 1)
     place = lax.axis_index("pen").astype(jnp.int32).reshape(1)
-    potential, slot_forces = pl.pallas_call(
-        functools.partial(solve_kernel, capacity, rows),
+    potential, field, rim = pl.pallas_call(
+        functools.partial(solve_kernel, rows),
         out_shape=(
             jax.ShapeDtypeStruct((rows, NG), jnp.float32),
-            jax.ShapeDtypeStruct((devices, tall_back, LANES), jnp.float32),
+            jax.ShapeDtypeStruct((rows // 8, 16, NG), jnp.float32),
+            jax.ShapeDtypeStruct((rows // 8, 16, LANES), jnp.float32),
         ),
-        in_specs=[smem] + [far] * 7,
-        out_specs=(far, vmem),
+        in_specs=[smem] + [far] * 5,
+        out_specs=(far, far, vmem),
         scratch_shapes=[
-            pltpu.SMEM((total + 8,), jnp.int32),
             pltpu.VMEM((rows + 16, NG), jnp.float32),
             pltpu.VMEM((rows + 16, NG), jnp.bfloat16),
             pltpu.VMEM((rows + 16, NG), jnp.bfloat16),
             pltpu.VMEM((rows // 8, 16, NG), jnp.float32),
-            pltpu.VMEM((rows // 8, 16, LANES), jnp.float32),
             pltpu.VMEM((rows, NG), jnp.float32),
             pltpu.VMEM((rows, NG), jnp.float32),
             pltpu.VMEM(gathered.shape, jnp.float32),
         ]
-        + arrived
         + table_scratch,
         compiler_params=params,
         name="solve",
-    )(place, header, received, spectrum, gathered, table_high, table_low, lines)
-    (returned,) = exchange((slot_forces,), plane_count, pen_count, 2)
+    )(place, spectrum, gathered, table_high, table_low, lines)
     forces = pl.pallas_call(
-        functools.partial(unpack_kernel, capacity),
+        functools.partial(pull_kernel, plane_count, pen_count, capacity),
         out_shape=jax.ShapeDtypeStruct((local_blocks, 2, block_len), jnp.float32),
-        in_specs=[smem, vmem],
+        in_specs=[smem] + [far] * 4,
         out_specs=vmem,
-        compiler_params=params,
-        name="unpack",
-    )(target, returned)
+        scratch_shapes=[
+            pltpu.VMEM((devices, tall_back, LANES), jnp.float32),
+            pltpu.VMEM((devices, tall_back, LANES), jnp.float32),
+            pltpu.SMEM(header.shape, jnp.int32),
+            pltpu.VMEM(received.shape, jnp.float32),
+            pltpu.VMEM(field.shape, jnp.float32),
+            pltpu.VMEM(rim.shape, jnp.float32),
+            pltpu.SemaphoreType.DMA((4,)),
+            pltpu.SemaphoreType.DMA((devices,)),
+            pltpu.SemaphoreType.DMA((devices,)),
+        ],
+        compiler_params=pltpu.CompilerParams(
+            collective_id=2, has_side_effects=True, vmem_limit_bytes=VMEM_LIMIT
+        ),
+        name="pull",
+    )(target, header, received, field, rim)
     return (potential[None], forces)
 
 

time: 100 us -> 93.1 us (0.931)
  Pallas kernels: 99.2 us -> 90.1 us
  local copies, waits for them, and re-layouts: 0 us -> 1.57 us
    pallas_call x2 -> x1, Pallas kernels: 33.5 us -> 21.5 us  [exchange(): pl.pallas_call(functools.partial(exchange_kernel, planes, pens, arrays),...]
    pallas_call x2, Pallas kernels: 35.3 us -> 44.7 us  [the longest x1 34.3 us: shards(): pl.pallas_call(functools.partial(pull_kernel, plane_count, pen_count, cap...]
    pallas_call x1, Pallas kernels: 20.2 us -> 13.6 us  [shards(): pl.pallas_call(functools.partial(deposit_kernel, capacity, rows), out_sha...]
    unnamed x0 -> x1, local copies, waits for them, and re-layouts: none -> 1.57 us
where the time goes in v2:
time: 93.1 us; the launch traced here: 92.3 us
  Pallas kernels  90.1 us (97%)
  local copies, waits for them, and re-layouts  1.57 us (2%)
    pallas_call x1, Pallas kernels, shards(): pl.pallas_call(functools.partial(pull_kernel, plane_count, pen_count, cap...  34.3 us
    pallas_call x1, Pallas kernels, exchange(): pl.pallas_call(functools.partial(exchange_kernel, planes, pens, arrays),...  21.5 us
    pallas_call x1, Pallas kernels, shards(): pl.pallas_call(functools.partial(deposit_kernel, capacity, rows), out_sha...  13.6 us
    pallas_call x1, Pallas kernels, shards(): pl.pallas_call(functools.partial(solve_kernel, rows), out_shape=(jax.Shap...  10.4 us
    pallas_call x1, Pallas kernels, share(): pl.pallas_call(functools.partial(share_kernel, pens), out_shape=jax.Shape...  7.25 us
    pallas_call x1, Pallas kernels, shards(): pl.pallas_call(functools.partial(pack_kernel, capacity), out_shape=(jax.S...  3.01 us

profile of v2, /device:TPU:0, one launch (start us, length us, event | category | flops | bytes accessed | tf_op | source)
XLA Modules:
  0.0 92.3 jit_solution(9821728078150973848)
XLA Ops:
  0.6 3.0 %pack.1 = (f32[32,32,128]{2,1,0:T(8,128)}, s32[32,1,128]{2,1,0:T(1,128)}, s32[128]{0:T(128)}) custom-call(s32[128]{0:T(128)} %bitcast.3, s32[128]{0:T(128)} %band_h.1, s32[128]{0:T(128)} %count_h.1, s32[128,128]{1,0:T(8,128)} %cells_h.1, f32[128,2,128]{2,1,0:T(2,128)} %offsets_h.1, f32[128,128]{1,0:T(8,128)} %charges_h.1), custom_call_target="tpu_custom_call" | custom-call | tf_op jit(solution)/shard_map/pack/pallas_call | solution.py:613
  3.7 21.5 %exchange.1 = (f32[32,32,128]{2,1,0:T(8,128)}, s32[32,1,128]{2,1,0:T(1,128)}) custom-call(f32[32,32,128]{2,1,0:T(8,128)} %get-tuple-element.12.refs_0_, s32[32,1,128]{2,1,0:T(1,128)} %get-tuple-element.13.refs_1_), custom_call_target="tpu_custom_call" | custom-call | tf_op jit(solution)/shard_map/exchange/pallas_call | solution.py:168
  25.2 13.6 %deposit.1 = (f32[256,1024]{1,0:T(8,128)}, f32[8,1024]{1,0:T(8,128)}) custom-call(s32[32,1,128]{2,1,0:T(1,128)} %get-tuple-element.14.header_h, f32[32,32,128]{2,1,0:T(8,128)} %get-tuple-element.15.recv_h, bf16[1024,1024]{1,0:T(8,128)(2,1)} %constant.10.clone.table_high_h, bf16[1024,1024]{1,0:T(8,128)(2,1)} %constant.11.clone.table_low_h, ...), custom_call_target="tpu_custom_call" | custom-call | tf_op jit(solution)/shard_map/deposit/pallas_call | solution.py:646
  38.8 7.3 %share.1.gathered_h = f32[4,8,1024]{2,1,0:T(8,128)} custom-call(f32[8,1024]{1,0:T(8,128)} %get-tuple-element.17.source), custom_call_target="tpu_custom_call" | custom-call | tf_op jit(solution)/shard_map/share/pallas_call | solution.py:223
  46.0 10.4 %solve.1 = (f32[256,1024]{1,0:T(8,128)}, f32[32,16,1024]{2,1,0:T(8,128)}, f32[32,16,128]{2,1,0:T(8,128)}) custom-call(s32[1]{0:T(128)} %bitcast.place, f32[256,1024]{1,0:T(8,128)} %get-tuple-element.16.spectrum_h, f32[4,8,1024]{2,1,0:T(8,128)} %share.1.gathered_h, bf16[1024,1024]{1,0:T(8,128)(2,1)} %constant.10.clone.table_high_h, ...), custom_call_target="tpu_custom_call" | custom-call | tf_op jit(solution)/shard_map/solve/pallas_call | solution.py:668
  56.4 34.3 %pull.1 = f32[128,2,128]{2,1,0:T(2,128)} custom-call(s32[128]{0:T(128)} %get-tuple-element.19.target, s32[32,1,128]{2,1,0:T(1,128)} %get-tuple-element.14.header_h, f32[32,32,128]{2,1,0:T(8,128)} %get-tuple-element.15.recv_h, f32[32,16,1024]{2,1,0:T(8,128)} %get-tuple-element.20.field_h, f32[32,16,128]{2,1,0:T(8,128)} %get-tuple-element.21.rim_h), custom_call_target="tpu_custom_call" | custom-call | tf_op jit(solution)/shard_map/pull/pallas_call | solution.py:690
  90.8 1.6 %copy.12 = f32[128,2,128]{2,1,0:T(2,128)} copy(f32[128,2,128]{2,1,0:T(2,128)} %pull.1) | data formatting | bytes 262144

commit v3 on v2

--- a/solution.py
+++ b/solution.py
@@ -182,59 +182,6 @@
     )(*values)
 
 
-def share_kernel(pens, source, target, send_sems, recv_sems, own_sem):
-    mine = lax.axis_index("pen")
-    plane = lax.axis_index("pln")
-    barrier = pltpu.get_barrier_semaphore()
-    own = pltpu.make_async_copy(source, target.at[mine], own_sem)
-    own.start()
-    for k in range(1, pens):
-        other = (plane, lax.rem(mine + k, pens))
-        pl.semaphore_signal(barrier, inc=1, device_id=other, device_id_type=pl.DeviceIdType.MESH)
-    pl.semaphore_wait(barrier, pens - 1)
-    sends = []
-    for k in range(1, pens):
-        copy = pltpu.make_async_remote_copy(
-            src_ref=source,
-            dst_ref=target.at[mine],
-            send_sem=send_sems.at[k],
-            recv_sem=recv_sems.at[k],
-            device_id=(plane, lax.rem(mine + k, pens)),
-            device_id_type=pl.DeviceIdType.MESH,
-        )
-        copy.start()
-        sends.append(copy)
-    for k in range(1, pens):
-        sends[k - 1].wait_send()
-        behind = lax.rem(mine - k + pens, pens)
-        pltpu.make_async_remote_copy(
-            src_ref=source,
-            dst_ref=target.at[behind],
-            send_sem=send_sems.at[k],
-            recv_sem=recv_sems.at[k],
-            device_id=(plane, behind),
-            device_id_type=pl.DeviceIdType.MESH,
-        ).wait_recv()
-    own.wait()
-
-
-def share(values, pens, number):
-    place = pl.BlockSpec(memory_space=pltpu.VMEM)
-    return pl.pallas_call(
-        functools.partial(share_kernel, pens),
-        out_shape=jax.ShapeDtypeStruct((pens,) + values.shape, values.dtype),
-        in_specs=[place],
-        out_specs=place,
-        scratch_shapes=[
-            pltpu.SemaphoreType.DMA((pens,)),
-            pltpu.SemaphoreType.DMA((pens,)),
-            pltpu.SemaphoreType.DMA,
-        ],
-        compiler_params=pltpu.CompilerParams(collective_id=number, has_side_effects=True, vmem_limit_bytes=VMEM_LIMIT),
-        name="share",
-    )(values)
-
-
 def live_list(header, live, capacity):
     def check(d, n):
         for j in range(capacity):
@@ -361,18 +308,9 @@
     edges[6:8] = jnp.zeros((2, NG), jnp.float32)
 
 
-def solve_kernel(rows, place, spectrum_h, gathered_h, table_high_h, table_low_h, lines_h, potential_h, field_h, rim,
-                 wave, hi, lo, field, potential, spectrum, gathered, table_high, table_low, lines, sems):
-    copies = fetch(
-        (lines_h, gathered_h, spectrum_h, table_high_h, table_low_h),
-        (lines, gathered, spectrum, table_high, table_low),
-        sems,
-    )
-    for copy in copies[:3]:
-        copy.wait()
+def solve(rows, mine, copies, potential_h, out_sem, rim, wave, hi, lo, field, potential, spectrum, gathered,
+          table_high, table_low, lines):
     pens = gathered.shape[0]
-    mine = place[0]
-
     def table(which):
         return lines[which * 8 : which * 8 + 8]
 
@@ -442,13 +380,13 @@
     hi[...] = high
     lo[...] = low
     width = 256
-    for copy in copies[3:5]:
+    for copy in copies:
         copy.wait()
     for n in range(NG // width):
         cols = slice(n * width, (n + 1) * width)
         wave[:, cols] = dot3(hi[...], lo[...], table_high[:, cols], table_low[:, cols])
     potential[...] = wave[8 : rows + 8]
-    out_copy = pltpu.make_async_copy(potential, potential_h, sems.at[7])
+    out_copy = pltpu.make_async_copy(potential, potential_h, out_sem)
     out_copy.start()
 
     def derive(t, carry):
@@ -470,7 +408,6 @@
         def _():
             field[t, 0:8, :] = along_x
             field[t, 8:16, :] = along_y
-            pltpu.make_async_copy(field.at[t], field_h.at[t], sems.at[6]).start()
 
         @pl.when(t > 0)
         def _():
@@ -482,16 +419,23 @@
         return carry
 
     lax.fori_loop(0, tiles + 1, derive, 0)
-    pltpu.make_async_copy(field, field_h, sems.at[6]).wait()
-    out_copy.wait()
-
-
-def pull_kernel(planes, pens, capacity, target, header_h, recv_h, field_h, rim_h, out,
-                forces, returned, header, recv, field, rim, sems, send_sems, recv_sems):
+    return out_copy
+
+
+def pull_kernel(planes, pens, capacity, rows, target, header_h, recv_h, spectrum_h, edges_h, table_high_h, table_low_h,
+                lines_h, potential_h, out, forces, returned, header, recv, field, rim, wave, hi, lo, potential,
+                spectrum, edges, gathered, table_high, table_low, lines, sems, send_sems, recv_sems,
+                edge_send_sems, edge_recv_sems):
     count = planes * pens
     me = lax.axis_index("pln") * pens + lax.axis_index("pen")
     barrier = pltpu.get_barrier_semaphore()
-    copies = fetch((field_h, header_h, recv_h, rim_h), (field, header, recv, rim), sems)
+    copies = fetch(
+        (edges_h, lines_h, spectrum_h, table_high_h, table_low_h, header_h, recv_h),
+        (edges, lines, spectrum, table_high, table_low, header, recv),
+        sems,
+    )
+    plane = lax.axis_index("pln")
+    mine = lax.axis_index("pen")
 
     def greet(k, carry):
         other = peer(lax.rem(me + k, count), pens)
@@ -499,7 +443,30 @@
         return carry
 
     lax.fori_loop(1, count, greet, 0)
-    for copy in copies:
+    for copy in copies[:3]:
+        copy.wait()
+    gathered[mine] = edges[...]
+    pl.semaphore_wait(barrier, count - 1)
+
+    def edge_copy(k, place, other):
+        return pltpu.make_async_remote_copy(
+            src_ref=edges,
+            dst_ref=gathered.at[place],
+            send_sem=edge_send_sems.at[k],
+            recv_sem=edge_recv_sems.at[k],
+            device_id=(plane, other),
+            device_id_type=pl.DeviceIdType.MESH,
+        )
+
+    for k in range(1, pens):
+        edge_copy(k, mine, lax.rem(mine + k, pens)).start()
+    for k in range(1, pens):
+        behind = lax.rem(mine - k + pens, pens)
+        edge_copy(k, mine, lax.rem(mine + k, pens)).wait_send()
+        edge_copy(k, behind, behind).wait_recv()
+    out_copy = solve(rows, mine, copies[3:5], potential_h, sems.at[7], rim, wave, hi, lo, field, potential, spectrum,
+                     gathered, table_high, table_low, lines)
+    for copy in copies[5:]:
         copy.wait()
     sub8 = lax.broadcasted_iota(jnp.int32, (8, LANES), 0)
     odd = (sub8 & 1) == 1
@@ -566,7 +533,6 @@
         )
 
     pull(lax.rem(me + 1, count))
-    pl.semaphore_wait(barrier, count - 1)
 
     def step(k, carry):
         to = lax.rem(me + k, count)
@@ -594,6 +560,7 @@
         return carry
 
     lax.fori_loop(0, out.shape[0], take, 0)
+    out_copy.wait()
 
 
 def shards(block_owner, block_band, block_count, cells, offsets, charges):
@@ -663,51 +630,41 @@
         compiler_params=params,
         name="deposit",
     )(header, received, table_high, table_low, lines)
-    gathered = share(edges, pen_count, 1)
-    place = lax.axis_index("pen").astype(jnp.int32).reshape(1)
-    potential, field, rim = pl.pallas_call(
-        functools.partial(solve_kernel, rows),
+    potential, forces = pl.pallas_call(
+        functools.partial(pull_kernel, plane_count, pen_count, capacity, rows),
         out_shape=(
             jax.ShapeDtypeStruct((rows, NG), jnp.float32),
-            jax.ShapeDtypeStruct((rows // 8, 16, NG), jnp.float32),
-            jax.ShapeDtypeStruct((rows // 8, 16, LANES), jnp.float32),
+            jax.ShapeDtypeStruct((local_blocks, 2, block_len), jnp.float32),
         ),
-        in_specs=[smem] + [far] * 5,
-        out_specs=(far, far, vmem),
-        scratch_shapes=[
-            pltpu.VMEM((rows + 16, NG), jnp.float32),
-            pltpu.VMEM((rows + 16, NG), jnp.bfloat16),
-            pltpu.VMEM((rows + 16, NG), jnp.bfloat16),
-            pltpu.VMEM((rows // 8, 16, NG), jnp.float32),
-            pltpu.VMEM((rows, NG), jnp.float32),
-            pltpu.VMEM((rows, NG), jnp.float32),
-            pltpu.VMEM(gathered.shape, jnp.float32),
-        ]
-        + table_scratch,
-        compiler_params=params,
-        name="solve",
-    )(place, spectrum, gathered, table_high, table_low, lines)
-    forces = pl.pallas_call(
-        functools.partial(pull_kernel, plane_count, pen_count, capacity),
-        out_shape=jax.ShapeDtypeStruct((local_blocks, 2, block_len), jnp.float32),
-        in_specs=[smem] + [far] * 4,
-        out_specs=vmem,
+        in_specs=[smem] + [far] * 7,
+        out_specs=(far, vmem),
         scratch_shapes=[
             pltpu.VMEM((devices, tall_back, LANES), jnp.float32),
             pltpu.VMEM((devices, tall_back, LANES), jnp.float32),
             pltpu.SMEM(header.shape, jnp.int32),
             pltpu.VMEM(received.shape, jnp.float32),
-            pltpu.VMEM(field.shape, jnp.float32),
-            pltpu.VMEM(rim.shape, jnp.float32),
-            pltpu.SemaphoreType.DMA((4,)),
+            pltpu.VMEM((rows // 8, 16, NG), jnp.float32),
+            pltpu.VMEM((rows // 8, 16, LANES), jnp.float32),
+            pltpu.VMEM((rows + 16, NG), jnp.float32),
+            pltpu.VMEM((rows + 16, NG), jnp.bfloat16),
+            pltpu.VMEM((rows + 16, NG), jnp.bfloat16),
+            pltpu.VMEM((rows, NG), jnp.float32),
+            pltpu.VMEM((rows, NG), jnp.float32),
+            pltpu.VMEM((8, NG), jnp.float32),
+            pltpu.VMEM((pen_count, 8, NG), jnp.float32),
+        ]
+        + table_scratch
+        + [
             pltpu.SemaphoreType.DMA((devices,)),
             pltpu.SemaphoreType.DMA((devices,)),
+            pltpu.SemaphoreType.DMA((pen_count,)),
+            pltpu.SemaphoreType.DMA((pen_count,)),
         ],
         compiler_params=pltpu.CompilerParams(
             collective_id=2, has_side_effects=True, vmem_limit_bytes=VMEM_LIMIT
         ),
         name="pull",
-    )(target, header, received, field, rim)
+    )(target, header, received, spectrum, edges, table_high, table_low, lines)
     return (potential[None], forces)
 
 

time: 93.1 us -> 90 us (0.967); the launches traced: 92.3 us -> 90.3 us
  Pallas kernels: 90.1 us -> 86.7 us
  local copies, waits for them, and re-layouts: 1.57 us -> 3 us
    pallas_call x2 -> x0, Pallas kernels: 17.7 us -> none  [the longest x1 10.4 us: shards(): pl.pallas_call(functools.partial(solve_kernel, rows), out_shape=(jax.Shap...]
    pallas_call x1, Pallas kernels: 34.3 us -> 43.1 us  [shards(): pl.pallas_call(functools.partial(pull_kernel, plane_count, pen_count, cap...]
    pallas_call x1, Pallas kernels: 13.6 us -> 19 us  [shards(): pl.pallas_call(functools.partial(deposit_kernel, capacity, rows), out_sha...]
    unnamed x1 -> x4, local copies, waits for them, and re-layouts: 1.57 us -> 3 us
where the time goes in v3:
time: 90 us; the launch traced here: 90.3 us
  Pallas kernels  86.7 us (96%)
  local copies, waits for them, and re-layouts  3 us (3%)
    pallas_call x1, Pallas kernels, shards(): pl.pallas_call(functools.partial(pull_kernel, plane_count, pen_count, cap...  43.1 us
    pallas_call x1, Pallas kernels, exchange(): pl.pallas_call(functools.partial(exchange_kernel, planes, pens, arrays),...  21.6 us
    pallas_call x1, Pallas kernels, shards(): pl.pallas_call(functools.partial(deposit_kernel, capacity, rows), out_sha...  19 us
    pallas_call x1, Pallas kernels, shards(): pl.pallas_call(functools.partial(pack_kernel, capacity), out_shape=(jax.S...  3.01 us
    unnamed x4, local copies, waits for them, and re-layouts  3 us

profile of v3, /device:TPU:0, one launch (start us, length us, event | category | flops | bytes accessed | tf_op | source)
XLA Modules:
  0.0 90.3 jit_solution(12061893170790314391)
XLA Ops:
  0.6 3.0 %pack.1 = (f32[32,32,128]{2,1,0:T(8,128)}, s32[32,1,128]{2,1,0:T(1,128)}, s32[128]{0:T(128)}) custom-call(s32[128]{0:T(128)} %bitcast.3, s32[128]{0:T(128)} %band_h.1, s32[128]{0:T(128)} %count_h.1, s32[128,128]{1,0:T(8,128)} %cells_h.1, f32[128,2,128]{2,1,0:T(2,128)} %offsets_h.1, f32[128,128]{1,0:T(8,128)} %charges_h.1), custom_call_target="tpu_custom_call" | custom-call | tf_op jit(solution)/shard_map/pack/pallas_call | solution.py:580
  3.6 21.6 %exchange.1 = (f32[32,32,128]{2,1,0:T(8,128)}, s32[32,1,128]{2,1,0:T(1,128)}) custom-call(f32[32,32,128]{2,1,0:T(8,128)} %get-tuple-element.12.refs_0_, s32[32,1,128]{2,1,0:T(1,128)} %get-tuple-element.13.refs_1_), custom_call_target="tpu_custom_call" | custom-call | tf_op jit(solution)/shard_map/exchange/pallas_call | solution.py:168
  25.2 19.0 %deposit.1 = (f32[256,1024]{1,0:T(8,128)}, f32[8,1024]{1,0:T(8,128)}) custom-call(s32[32,1,128]{2,1,0:T(1,128)} %get-tuple-element.14.header_h, f32[32,32,128]{2,1,0:T(8,128)} %get-tuple-element.15.recv_h, bf16[1024,1024]{1,0:T(8,128)(2,1)} %constant.6.clone.table_high_h, bf16[1024,1024]{1,0:T(8,128)(2,1)} %constant.7.clone.table_low_h, ...), custom_call_target="tpu_custom_call" | custom-call | tf_op jit(solution)/shard_map/deposit/pallas_call | solution.py:613
  44.2 43.1 %pull.1 = (f32[256,1024]{1,0:T(8,128)}, f32[128,2,128]{2,1,0:T(2,128)}) custom-call(s32[128]{0:T(128)} %get-tuple-element.11.target, s32[32,1,128]{2,1,0:T(1,128)} %get-tuple-element.14.header_h, f32[32,32,128]{2,1,0:T(8,128)} %get-tuple-element.15.recv_h, f32[256,1024]{1,0:T(8,128)} %get-tuple-element.16.spectrum_h, f32[8,1024]{1,0:T(8,128)} %get-tuple-element.17.edges_h, ...), custom_call_target="tpu_custom_call" | custom-call | tf_op jit(solution)/shard_map/pull/pallas_call | solution.py:633
  87.3 0.0 copy-start
  87.3 2.3 %copy.13 = f32[1,256,1024]{2,1,0:T(8,128)} copy(f32[1,256,1024]{2,1,0:T(8,128)} %bitcast.2) | data formatting | bytes 2097152
  89.7 0.0 copy-done
  89.7 0.7 copy.14
Async XLA Ops:
  87.3 2.4 %copy-start = (f32[128,2,128]{2,1,0:T(2,128)S(1)}, f32[128,2,128]{2,1,0:T(2,128)}, u32[]{:S(2)}) copy-start(f32[128,2,128]{2,1,0:T(2,128)} %get-tuple-element.23) | copy-start | bytes 393220

commit v4 on v3

--- a/solution.py
+++ b/solution.py
@@ -14,7 +14,7 @@
 CHUNKS = NG // LANES
 screening = 2e-05
 VMEM_LIMIT = 62 * 1024 * 1024
-UNROLL = 4
+UNROLL = 8
 
 
 def round_up(value, step):

time: 90 us -> 86.5 us (0.961)
  Pallas kernels: 86.7 us -> 82.5 us
    pallas_call x1, Pallas kernels: 19 us -> 10.5 us  [shards(): pl.pallas_call(functools.partial(deposit_kernel, capacity, rows), out_sha...]
    pallas_call x1, Pallas kernels: 43.1 us -> 47.4 us  [shards(): pl.pallas_call(functools.partial(pull_kernel, plane_count, pen_count, cap...]
where the time goes in v4:
time: 86.5 us; the launch traced here: 86.1 us
  Pallas kernels  82.5 us (95%)
  local copies, waits for them, and re-layouts  3 us (3%)
    pallas_call x1, Pallas kernels, shards(): pl.pallas_call(functools.partial(pull_kernel, plane_count, pen_count, cap...  47.4 us
    pallas_call x1, Pallas kernels, exchange(): pl.pallas_call(functools.partial(exchange_kernel, planes, pens, arrays),...  21.6 us
    pallas_call x1, Pallas kernels, shards(): pl.pallas_call(functools.partial(deposit_kernel, capacity, rows), out_sha...  10.5 us
    pallas_call x1, Pallas kernels, shards(): pl.pallas_call(functools.partial(pack_kernel, capacity), out_shape=(jax.S...  3.01 us
    unnamed x4, local copies, waits for them, and re-layouts  3 us

profile of v4, /device:TPU:0, one launch (start us, length us, event | category | flops | bytes accessed | tf_op | source)
XLA Modules:
  0.0 86.1 jit_solution(1123199572463649433)
XLA Ops:
  0.6 3.0 %pack.1 = (f32[32,32,128]{2,1,0:T(8,128)}, s32[32,1,128]{2,1,0:T(1,128)}, s32[128]{0:T(128)}) custom-call(s32[128]{0:T(128)} %bitcast.3, s32[128]{0:T(128)} %band_h.1, s32[128]{0:T(128)} %count_h.1, s32[128,128]{1,0:T(8,128)} %cells_h.1, f32[128,2,128]{2,1,0:T(2,128)} %offsets_h.1, f32[128,128]{1,0:T(8,128)} %charges_h.1), custom_call_target="tpu_custom_call" | custom-call | tf_op jit(solution)/shard_map/pack/pallas_call | solution.py:580
  3.6 21.6 %exchange.1 = (f32[32,32,128]{2,1,0:T(8,128)}, s32[32,1,128]{2,1,0:T(1,128)}) custom-call(f32[32,32,128]{2,1,0:T(8,128)} %get-tuple-element.12.refs_0_, s32[32,1,128]{2,1,0:T(1,128)} %get-tuple-element.13.refs_1_), custom_call_target="tpu_custom_call" | custom-call | tf_op jit(solution)/shard_map/exchange/pallas_call | solution.py:168
  25.2 10.5 %deposit.1 = (f32[256,1024]{1,0:T(8,128)}, f32[8,1024]{1,0:T(8,128)}) custom-call(s32[32,1,128]{2,1,0:T(1,128)} %get-tuple-element.14.header_h, f32[32,32,128]{2,1,0:T(8,128)} %get-tuple-element.15.recv_h, bf16[1024,1024]{1,0:T(8,128)(2,1)} %constant.6.clone.table_high_h, bf16[1024,1024]{1,0:T(8,128)(2,1)} %constant.7.clone.table_low_h, ...), custom_call_target="tpu_custom_call" | custom-call | tf_op jit(solution)/shard_map/deposit/pallas_call | solution.py:613
  35.7 47.4 %pull.1 = (f32[256,1024]{1,0:T(8,128)}, f32[128,2,128]{2,1,0:T(2,128)}) custom-call(s32[128]{0:T(128)} %get-tuple-element.11.target, s32[32,1,128]{2,1,0:T(1,128)} %get-tuple-element.14.header_h, f32[32,32,128]{2,1,0:T(8,128)} %get-tuple-element.15.recv_h, f32[256,1024]{1,0:T(8,128)} %get-tuple-element.16.spectrum_h, f32[8,1024]{1,0:T(8,128)} %get-tuple-element.17.edges_h, ...), custom_call_target="tpu_custom_call" | custom-call | tf_op jit(solution)/shard_map/pull/pallas_call | solution.py:633
  83.1 0.0 copy-start
  83.1 2.3 %copy.13 = f32[1,256,1024]{2,1,0:T(8,128)} copy(f32[1,256,1024]{2,1,0:T(8,128)} %bitcast.2) | data formatting | bytes 2097152
  85.5 0.0 copy-done
  85.5 0.7 copy.14
Async XLA Ops:
  83.1 2.4 %copy-start = (f32[128,2,128]{2,1,0:T(2,128)S(1)}, f32[128,2,128]{2,1,0:T(2,128)}, u32[]{:S(2)}) copy-start(f32[128,2,128]{2,1,0:T(2,128)} %get-tuple-element.23) | copy-start | bytes 393220
